TPU v7x, 128 devices: a whole 4x4x4 slice. The times are simulated.
128 devices in a mesh: row: 8 (over z, core), col: 16 (over x, y).
Axes of the slice: x: 4, y: 4, z: 4, core: 2. Of those that a mesh axis runs over, the one named last changes fastest.
Arguments:
- offsets: float32 [8, 16, 2, 256], P('row', 'col'), may hold values from 0 to 1
- point_order: int32 [8, 16, 256], P('row', 'col'), may hold values from 0 to 255, each once within a row
- nugget: float32 [8, 16, 256], P('row', 'col'), may hold values from 1 to 4
- interp: float32 [8, 16, 128, 128], P('row', 'col'), may hold values from -0.5 to 0.5
Outputs:
- root_work: float32 [16384, 16384], P('row', 'col')
Inputs may be any that keep to these rules, and one draw needn't show every extreme that they name: `point_order`: each row lists every point of its box once; its first 128 entries name the box's skeleton points.
All inputs are finite; a program needn't handle non-finite values.
Results may differ from a plain program's by a relative error of at most 0.0001.
Values sent between devices are 32-bit elements; how exact they have to be, the bound alone decides.
A program may use at most 128 MiB of HBM per device.

v0:
```python
import jax
import jax.numpy as jnp
from jax import lax
from jax.experimental import pallas as pl
from jax.experimental.pallas import tpu as pltpu
from jax.sharding import PartitionSpec as P

SB = 1024


kernel_amp = 0.015625
kernel_len = 0.5


def factor128(a):
    n = a.shape[0]
    G = n // 8
    rows = [a[8*g:8*g+8] for g in range(G)]
    lane = lax.broadcasted_iota(jnp.int32, (8, n), 1)
    sub = lax.broadcasted_iota(jnp.int32, (8, n), 0)
    w = [(lane == sub + 8*g).astype(jnp.float32) for g in range(G)]
    def srow(v, t):
        return jnp.broadcast_to(v[t:t+1], (8, n))
    def lcol(v, t):
        return jnp.broadcast_to(v[:, t:t+1], (8, n))
    us, ws = [], []
    for p in range(G):
        q, qw = rows[p], w[p]
        cols = [lcol(q, 8*p+t) for t in range(8)]
        u, uw, dv = q, qw, None
        for t in range(8):
            pr, pw = srow(q, t), srow(qw, t)
            d = srow(cols[t], t)
            here = sub == t
            u = pr if t == 0 else jnp.where(here, pr, u)
            uw = pw if t == 0 else jnp.where(here, pw, uw)
            dv = d if t == 0 else jnp.where(here, d, dv)
            m = jnp.where(here, 0.0, cols[t]) * (1.0 / d)
            q = q - m * pr
            qw = qw - m * pw
            for v in range(t + 1, 8):
                cols[v] = cols[v] - m * srow(cols[v], t)
        r = lax.rsqrt(dv)
        us.append(jnp.where(lane >= sub + 8*p, u * r, 0.0))
        ws.append(uw * r)
        inv = 1.0 / dv
        z, zw = q * inv, qw * inv
        zs = [srow(z, t) for t in range(8)]
        zws = [srow(zw, t) for t in range(8)]
        for g in range(p + 1, G):
            cg = [lcol(rows[g], 8*p+t) for t in range(8)]
            x = [cg[t] * zs[t] for t in range(8)]
            y = [cg[t] * zws[t] for t in range(8)]
            rows[g] = rows[g] - (((x[0]+x[1])+(x[2]+x[3]))+((x[4]+x[5])+(x[6]+x[7])))
            w[g] = w[g] - (((y[0]+y[1])+(y[2]+y[3]))+((y[4]+y[5])+(y[6]+y[7])))
    return jnp.concatenate(us, 0), jnp.concatenate(ws, 0)


def split(x):
    hi = x.astype(jnp.bfloat16)
    return hi, (x - hi.astype(jnp.float32)).astype(jnp.bfloat16)


def dot3(a, b, dims):
    def one(x, y):
        return lax.dot_general(x, y, (dims, ((), ())), preferred_element_type=jnp.float32)

    return one(a[0], b[1]) + one(a[1], b[0]) + one(a[0], b[0])


NN = ((1,), (0,))
TN = ((0,), (0,))
NT = ((1,), (1,))


def box_kernel(pack_ref, out_ref, near, ea, f, fs, g, mat, acc, tx, rx, fx, dd, ps, pr, ks, kr, xs, xr):
    row_at = lax.axis_index("row")
    col_at = lax.axis_index("col")
    row_count = lax.axis_size("row")
    col_count = lax.axis_size("col")

    def inside(a, b):
        r, c = row_at + a, col_at + b
        return (r >= 0) & (r < row_count) & (c >= 0) & (c < col_count)

    def colour(a, b):
        return 2 * ((row_at + a + 2) % 2) + (col_at + b + 2) % 2

    def unslot(n):
        return n // 3 - 1, n % 3 - 1

    def near_pair(a, b):
        return (a >= -1) & (a <= 1) & (b >= -1) & (b <= 1)

    def loop(body, low=0, high=9):
        def step(n, _):
            body(n)
            return 0

        lax.fori_loop(low, high, step, 0)

    def copy(src, dst, send, recv, a, b):
        return pltpu.make_async_remote_copy(
            src_ref=src,
            dst_ref=dst,
            send_sem=send,
            recv_sem=recv,
            device_id=(row_at + a, col_at + b),
            device_id_type=pl.DeviceIdType.MESH,
        )

    def neighbours(body):
        def each(n):
            a, b = unslot(n)

            @pl.when((n != 4) & inside(a, b))
            def _():
                body(n, a, b)

        loop(each)

    def pack_copy(n, a, b):
        return copy(pack_ref, near.at[8 - n], ps.at[n], pr.at[8 - n], a, b)

    def k_copy(n, e, a, b):
        return copy(tx.at[e], rx.at[8 - n, e], ks.at[n, e], kr.at[8 - n, e], a, b)

    def x_copy(h, o):
        a, b = unslot(h)
        return copy(fs.at[o], fx.at[h - 5, o], xs.at[h - 5, o], xr.at[h - 5, o], -a, -b)

    barrier = pltpu.get_barrier_semaphore()

    def greet(n, a, b):
        pl.semaphore_signal(
            barrier,
            inc=1,
            device_id=(row_at + a, col_at + b),
            device_id_type=pl.DeviceIdType.MESH,
        )

    neighbours(greet)
    tall = 1 + lax.min(row_at, 1) + lax.min(row_count - 1 - row_at, 1)
    wide = 1 + lax.min(col_at, 1) + lax.min(col_count - 1 - col_at, 1)
    pl.semaphore_wait(barrier, tall * wide - 1)
    neighbours(lambda n, a, b: pack_copy(n, a, b).start())

    own = pack_ref[128:136]
    own_interp = split(pack_ref[0:128])
    my_colour = colour(0, 0)
    eye = lax.broadcasted_iota(jnp.int32, (128, 128), 0) == lax.broadcasted_iota(
        jnp.int32, (128, 128), 1
    )

    def start_block(source, here, slot):
        where = source[128:136].T
        parts = []
        for s in range(2):
            line = []
            for t in range(2):
                gap_row = where[:, s : s + 1] - own[t : t + 1]
                gap_col = where[:, 2 + s : 3 + s] - own[2 + t : 3 + t]
                square = gap_row * gap_row + gap_col * gap_col
                block = kernel_amp * jnp.exp(-jnp.sqrt(square) / kernel_len)
                if here and s == t:
                    block = block + jnp.where(eye, own[4 + s : 5 + s], 0.0)
                line.append(block)
            parts.append(jnp.concatenate(line, axis=1))
        ea[slot] = parts[1] - dot3(split(source[0:128]), split(parts[0]), TN)

    start_block(pack_ref, True, 4)
    mat[...] = ea[4, :, 128:] - dot3(split(ea[4, :, :128]), own_interp, NN)

    def start(n, a, b):
        pack_copy(8 - n, -a, -b).wait_recv()
        start_block(near.at[n], False, n)

    neighbours(start)

    def stage(k):
        @pl.when(my_colour == k)
        def _():
            tx[4] = factor128(mat[...])[1]

            def outgoing(e):
                ea_, eb_ = unslot(e)

                def dispatch(n, a, b):
                    @pl.when(near_pair(ea_ - a, eb_ - b))
                    def _():
                        k_copy(n, e, a, b).start()

                @pl.when(e == 4)
                def _():
                    neighbours(dispatch)

                @pl.when((e != 4) & inside(ea_, eb_) & (colour(ea_, eb_) < k))
                def _():
                    tx[e] = dot3(split(tx[4]), split(g[e]), NT)
                    neighbours(dispatch)

            outgoing(4)
            loop(lambda e: pl.when(e != 4)(lambda: outgoing(e)))

        def arrive(o):
            oa, ob = unslot(o)

            @pl.when(inside(oa, ob) & (colour(oa, ob) == k))
            def _():
                @pl.when(o == 4)
                def _():
                    acc[...] = dot3(split(tx[4]), split(ea[4]), NN)

                @pl.when(o != 4)
                def _():
                    k_copy(8 - o, 4, -oa, -ob).wait_recv()
                    acc[...] = dot3(split(rx[o, 4]), split(ea[o]), NN)

                def term(e):
                    ea_, eb_ = unslot(e)
                    va, vb = oa + ea_, ob + eb_

                    @pl.when((e != 4) & near_pair(va, vb) & inside(va, vb) & (colour(va, vb) < k))
                    def _():
                        right = split(f[(va + 1) * 3 + vb + 1])

                        @pl.when(o == 4)
                        def _():
                            acc[...] -= dot3(split(tx[e]), right, NN)

                        @pl.when(o != 4)
                        def _():
                            k_copy(8 - o, e, -oa, -ob).wait_recv()
                            acc[...] -= dot3(split(rx[o, e]), right, NN)

                loop(term)
                f[o] = acc[...]
                fs[o] = acc[:, :128]

                @pl.when(my_colour > k)
                def _():
                    new = acc[:, 128:] - dot3(split(acc[:, :128]), own_interp, NN)
                    g[o] = new
                    new2 = split(new)
                    mat[...] -= dot3(new2, new2, TN)

                def forward(h):
                    ha, hb = unslot(h)

                    @pl.when(inside(-ha, -hb) & near_pair(oa + ha, ob + hb))
                    def _():
                        x_copy(h, o).start()

                loop(forward, 5, 9)

        loop(arrive)

    loop(stage, 0, 4)

    def centre(o):
        oa, ob = unslot(o)

        @pl.when(inside(oa, ob))
        def _():
            part = split(fs[o])
            acc[:, :128] -= dot3(part, part, TN)

    acc[:, :128] = jnp.where(eye, own[4:5], 0.0)
    loop(centre)
    dd[0] = acc[:, :128]

    def pair(h):
        ha, hb = unslot(h)
        acc[:, :128] = jnp.zeros((128, 128), jnp.float32)

        @pl.when(inside(ha, hb))
        def _():
            def term(o):
                oa, ob = unslot(o)
                va, vb = oa - ha, ob - hb

                @pl.when(inside(oa, ob) & near_pair(va, vb))
                def _():
                    e = (va + 1) * 3 + vb + 1
                    x_copy(h, e).wait_recv()
                    acc[:, :128] -= dot3(split(fs[o]), split(fx[h - 5, e]), TN)

            loop(term)

        dd[h - 4] = acc[:, :128]
        dd[h] = acc[:, :128].T

    loop(pair, 5, 9)

    lane = lax.broadcasted_iota(jnp.int32, (8, 128), 1)

    def gather(items):
        value = jnp.zeros((8, 128), jnp.float32)
        for source, start, place, size in items:
            moved = pltpu.roll(source, (place - start) % 128, 1)
            value = jnp.where((lane >= place) & (lane < place + size), moved, value)
        return value

    heads = [dd[n, 0:8] for n in range(9)]
    corner = [(heads[n], 0, 8 + 8 * n, 8) for n in range(9)]
    wide_rows = [
        gather([(heads[n], 16 * r, 16 + 16 * n, 16) for n in range(7)]) for r in range(8)
    ]
    more_rows = [
        gather(
            [(heads[7 + n], 16 * r, 16 * n, 16) for n in range(2)]
            + [(own, 16 * r, 32, 16), (own, 0, 56, 8)]
        )
        for r in range(8)
    ]
    corner = gather(corner)
    for c in range(16):
        rows = slice(8 * c, 8 * c + 8)
        group = [dd[n, rows] for n in range(9)]
        turn = group[1:]
        for bit in range(3):
            step = 1 << bit
            upper = ((lane // 16) // step) % 2 == 1
            for n in range(8):
                if n & step:
                    continue
                low, high = turn[n], turn[n + step]
                turn[n] = jnp.where(upper, pltpu.roll(high, 16 * step, 1), low)
                turn[n + step] = jnp.where(upper, high, pltpu.roll(low, 128 - 16 * step, 1))
        side = gather([(own, 8 * c, 48, 8)] + [(group[n], 0, 64 + 8 * n, 8) for n in range(8)])
        tail = jnp.where(lane < 8, group[8], corner)
        for r in range(8):
            dest = 16 * r + c
            out_ref[dest, 0] = turn[r]
            first = group[0] if r == 0 else pltpu.roll(group[0], 128 - 16 * r, 1)
            out_ref[dest, 1] = jnp.where(lane < 16, first, wide_rows[r])
            out_ref[dest, 2] = jnp.where((lane < 48) | ((lane >= 56) & (lane < 64)), more_rows[r], side)
            out_ref[dest, 3] = tail

    def finish(n, a, b):
        pack_copy(n, a, b).wait_send()

        def each(e):
            ea_, eb_ = unslot(e)
            is_sent = (e == 4) | (inside(ea_, eb_) & (colour(ea_, eb_) < my_colour))

            @pl.when(is_sent & near_pair(ea_ - a, eb_ - b))
            def _():
                k_copy(n, e, a, b).wait_send()

        loop(each)

    neighbours(finish)

    def finish_x(h):
        ha, hb = unslot(h)

        def each(o):
            oa, ob = unslot(o)

            @pl.when(inside(-ha, -hb) & inside(oa, ob) & near_pair(oa + ha, ob + hb))
            def _():
                x_copy(h, o).wait_send()

        loop(each)

    loop(finish_x, 5, 9)


def box_phase(pack):
    block = (128, 128)
    return pl.pallas_call(
        box_kernel,
        out_shape=jax.ShapeDtypeStruct((128, 4, 8, 128), jnp.float32),
        in_specs=[pl.BlockSpec(memory_space=pltpu.VMEM)],
        out_specs=pl.BlockSpec(memory_space=pltpu.VMEM),
        scratch_shapes=[
            pltpu.VMEM((9, 136, 128), jnp.float32),
            pltpu.VMEM((9, 128, 256), jnp.float32),
            pltpu.VMEM((9, 128, 256), jnp.float32),
            pltpu.VMEM((9,) + block, jnp.float32),
            pltpu.VMEM((9,) + block, jnp.float32),
            pltpu.VMEM(block, jnp.float32),
            pltpu.VMEM((128, 256), jnp.float32),
            pltpu.VMEM((9,) + block, jnp.float32),
            pltpu.VMEM((9, 9) + block, jnp.float32),
            pltpu.VMEM((4, 9) + block, jnp.float32),
            pltpu.VMEM((9,) + block, jnp.float32),
            pltpu.SemaphoreType.DMA((9,)),
            pltpu.SemaphoreType.DMA((9,)),
            pltpu.SemaphoreType.DMA((9, 9)),
            pltpu.SemaphoreType.DMA((9, 9)),
            pltpu.SemaphoreType.DMA((4, 9)),
            pltpu.SemaphoreType.DMA((4, 9)),
        ],
        compiler_params=pltpu.CompilerParams(
            collective_id=0, has_side_effects=True, vmem_limit_bytes=40 * 2**20
        ),
    )(pack)


def cat_right(x):
    hi, lo = split(x)
    return jnp.concatenate([hi, hi, lo], axis=0)


def cat_left(x):
    hi, lo = split(x)
    return jnp.concatenate([hi, lo, hi], axis=1)


def mm(a, b):
    return lax.dot_general(a, b, (NN, ((), ())), preferred_element_type=jnp.float32)


OFFSETS = [0, 1, 15, 16, 17, -1, -15, -16, -17]


def apart():
    return lax.broadcasted_iota(jnp.int32, (128, 128), 0) - lax.broadcasted_iota(
        jnp.int32, (128, 128), 1
    )


def root_block(row_x, row_y, col_x, col_y, lines):
    gap_x = row_x - col_x
    gap_y = row_y - col_y
    square = gap_x * gap_x + gap_y * gap_y
    distance = square * lax.rsqrt(jnp.maximum(square, 1e-36))
    value = jnp.exp2(distance * (-1.4426950408889634 / kernel_len) - 6.0)
    gap = apart()
    extra = jnp.zeros((128, 128), jnp.float32)
    for n in range(9):
        extra = jnp.where(gap == OFFSETS[n], lines[n], extra)
    return value + extra


def shifted_line(line, n):
    return pltpu.roll(line, -OFFSETS[n] % 128, 1) if n > 4 else line


def root_kernel(flag_ref, turned, lead_ref, hi_ref, lo_ref, work, diag, wcur, left, right, wt, tab):
    count = SB // 128
    width = 3 * SB
    chunk = 256
    row = lax.broadcasted_iota(jnp.int32, (128, SB), 0)
    col = lax.broadcasted_iota(jnp.int32, (128, SB), 1)

    def rows_of(i):
        return pl.ds(pl.multiple_of(i * 128, 128), 128)

    for l in range(8):
        for n in range(9):
            place = 64 + 8 * n
            line = turned[16 + l, place : place + 8] if n < 8 else turned[24 + l, 0:8]
            tab[0, l, n] = shifted_line(line, n)
            tab[1, l, n] = shifted_line(turned[24 + l, 8 + 8 * n : 16 + 8 * n], n)

    def assemble(k, _):
        for l in range(8):
            for which in range(2):
                place = 48 + 8 * which + l
                lines = [tab[which, l, n, pl.ds(k, 1)] for n in range(9)]
                start = SB * (1 - which) + 128 * l
                work[rows_of(k), start : start + 128] = root_block(
                    lead_ref[k, 0],
                    lead_ref[k, 1],
                    turned[16, place : place + 1],
                    turned[18, place : place + 1],
                    lines,
                )
        return 0

    lax.fori_loop(0, count, assemble, 0)
    for i in range(count):
        work[128 * i : 128 * i + 128, 2 * SB :] = jnp.where(col == row + 128 * i, 1.0, 0.0)
    work[SB:] = jnp.zeros((128, width), jnp.float32)
    diag[...] = work[:128, :128]
    wcur[...] = jnp.zeros((128, 384), jnp.bfloat16)

    def scale(p):
        here = rows_of(p)
        for c in range(width // chunk):
            cols = slice(c * chunk, c * chunk + chunk)
            new = mm(wcur[...], cat_right(work[here, cols]))
            work[here, cols] = new
            right[:, cols] = cat_right(new)
            for j in range(chunk // 128):
                n = c * (chunk // 128) + j
                if n < count:
                    part = jnp.where(p < n, new[:, 128 * j : 128 * j + 128], 0.0)
                    left[128 * n : 128 * n + 128] = cat_left(part.T)

    def step(i, _):
        p = jnp.where(i == 0, count, i - 1)
        scale(p)
        for c in range(width // chunk):
            cols = slice(c * chunk, c * chunk + chunk)
            work[:SB, cols] -= mm(left[...], right[:, cols])
        w = factor128(diag[...])[1]
        wcur[...] = cat_left(w)
        here, after = rows_of(i), rows_of(i + 1)
        u = mm(wcur[...], cat_right(work[here, after]))
        diag[...] = work[after, after] - mm(cat_left(u.T), cat_right(u))
        return 0

    lax.fori_loop(0, count, step, 0)
    last = rows_of(count - 1)
    for c in range(SB // chunk, width // chunk):
        cols = slice(c * chunk, c * chunk + chunk)
        work[last, cols] = mm(wcur[...], cat_right(work[last, cols]))

    def flip(i, _):
        here = rows_of(i)

        @pl.when(flag_ref[0] == 1)
        def _():
            work[here, SB : 2 * SB] = jnp.where(col == row + 128 * i, -1.0, 0.0)

        hi, lo = split(work[here, SB : 2 * SB])
        right[0:128, :SB] = hi
        hi_ref[here] = hi
        lo_ref[here] = lo
        for j in range(count):
            hi, lo = split(work[here, 2 * SB + 128 * j : 2 * SB + 128 * j + 128].T)
            there = slice(128 * j, 128 * j + 128)
            wt[0, there, here] = hi
            wt[1, there, here] = lo
        return 0

    lax.fori_loop(0, count, flip, 0)
    for c in range(SB // chunk):
        cols = slice(c * chunk, c * chunk + chunk)
        y_hi, y_lo = hi_ref[:, cols], lo_ref[:, cols]
        for m in range(4):
            some = slice(m * 256, m * 256 + 256)
            deep = slice(m * 256, SB)
            w_hi, w_lo = wt[0, some, deep], wt[1, some, deep]
            work[some, cols] = (
                mm(w_hi, y_lo[m * 256 :]) + mm(w_lo, y_hi[m * 256 :]) + mm(w_hi, y_hi[m * 256 :])
            )
        for m in range(4):
            some = slice(m * 256, m * 256 + 256)
            hi, lo = split(work[some, cols])
            hi_ref[some, cols] = hi
            lo_ref[some, cols] = lo


def root_solve(flag, turned, lead):
    return pl.pallas_call(
        root_kernel,
        out_shape=[jax.ShapeDtypeStruct((SB, SB), jnp.bfloat16)] * 2,
        in_specs=[
            pl.BlockSpec(memory_space=pltpu.SMEM),
            pl.BlockSpec(memory_space=pltpu.VMEM),
            pl.BlockSpec(memory_space=pltpu.VMEM),
        ],
        out_specs=[pl.BlockSpec(memory_space=pltpu.VMEM)] * 2,
        scratch_shapes=[
            pltpu.VMEM((SB + 128, 3 * SB), jnp.float32),
            pltpu.VMEM((128, 128), jnp.float32),
            pltpu.VMEM((128, 384), jnp.bfloat16),
            pltpu.VMEM((SB, 384), jnp.bfloat16),
            pltpu.VMEM((384, 3 * SB), jnp.bfloat16),
            pltpu.VMEM((2, SB, SB), jnp.bfloat16),
            pltpu.VMEM((2, 8, 9, 8, 128), jnp.float32),
        ],
        compiler_params=pltpu.CompilerParams(vmem_limit_bytes=48 * 2**20),
    )(flag, turned, lead)


def final_kernel(at_ref, turned, rows_ref, hi_ref, lo_ref, out_ref, tab, buffer):
    rows, cols = out_ref.shape
    s = pl.program_id(0)

    @pl.when(s == 0)
    def _():
        for l in range(8):
            for n in range(9):
                place = 16 * (n - 1)
                line = turned[l, place : place + 16] if n else turned[8 + l, 0:16]
                tab[0, l, n] = shifted_line(line, n)
                place = 16 * n + 16
                line = turned[8 + l, place : place + 16] if n < 7 else turned[16 + l, place - 128 : place - 112]
                tab[1, l, n] = shifted_line(line, n)

    def piece(which, k, l):
        place = 48 + 8 * which + l
        lines = [tab[which, l, n, pl.ds(k, 1)] for n in range(9)]
        return root_block(
            rows_ref[k, 0],
            rows_ref[k, 1],
            turned[16, place : place + 1],
            turned[18, place : place + 1],
            lines,
        )

    ahead = lax.min(s, pl.num_programs(0) - 2)
    now = lax.max(s - 1, 0)
    slot, other = s % 2, (s + 1) % 2
    first = at_ref[0] * (rows * (pl.num_programs(0) - 1)) + now * rows
    start = at_ref[1] * cols
    row = lax.broadcasted_iota(jnp.int32, (128, 128), 0)
    col = lax.broadcasted_iota(jnp.int32, (128, 128), 1)
    for c in range(cols // 256):
        some = slice(c * 256, c * 256 + 256)
        for half in range(2):
            for l in (2 * c, 2 * c + 1):
                hi, lo = split(piece(1, 2 * ahead + half, l))
                buffer[slot, 0, 128 * half : 128 * half + 128, 128 * l : 128 * l + 128] = hi
                buffer[slot, 1, 128 * half : 128 * half + 128, 128 * l : 128 * l + 128] = lo
        x_hi, x_lo = buffer[other, 0], buffer[other, 1]
        hi, lo = hi_ref[:, some], lo_ref[:, some]
        product = mm(x_hi, lo) + mm(x_lo, hi) + mm(x_hi, hi)
        for half in range(2):
            for l in (2 * c, 2 * c + 1):
                base = piece(0, 2 * now + half, l)
                part = product[128 * half : 128 * half + 128, 128 * (l % 2) : 128 * (l % 2) + 128]
                value = jnp.where(at_ref[1] == 0, 0.0, base) - part
                here = first + 128 * half + row
                there = start + 128 * l + col
                out_ref[128 * half : 128 * half + 128, 128 * l : 128 * l + 128] = jnp.where(
                    (here < SB) & (there > here), 0.0, value
                )


def final_product(at, turned, rows_wide, hi, lo):
    block = 256
    steps = 2048 // block
    cols = hi.shape[1]

    def whole(x):
        return pl.BlockSpec(x.shape, lambda i: (0,) * x.ndim)

    return pl.pallas_call(
        final_kernel,
        grid=(steps + 1,),
        out_shape=jax.ShapeDtypeStruct((steps * block, cols), jnp.float32),
        in_specs=[
            pl.BlockSpec(memory_space=pltpu.SMEM),
            whole(turned),
            whole(rows_wide),
            whole(hi),
            whole(lo),
        ],
        out_specs=pl.BlockSpec((block, cols), lambda i: (lax.max(i - 1, 0), 0)),
        scratch_shapes=[
            pltpu.VMEM((2, 8, 9, 16, 128), jnp.float32),
            pltpu.VMEM((2, 2, block, SB), jnp.bfloat16),
        ],
        compiler_params=pltpu.CompilerParams(vmem_limit_bytes=48 * 2**20),
    )(at, turned, rows_wide, hi, lo)


def root_phase(outgoing, row_at, col_at):
    arrived = lax.all_to_all(
        outgoing.reshape(128, 32, 128), ("row", "col"), split_axis=0, concat_axis=0, tiled=True
    )
    turned = jnp.transpose(arrived, (1, 2, 0))

    def wide(start, size):
        part = jnp.stack([turned[16, start : start + size], turned[18, start : start + size]], axis=1)
        return jnp.broadcast_to(part[:, :, :, None], part.shape + (128,))

    flag = (col_at == 0).astype(jnp.int32)
    hi, lo = root_solve(flag[None], turned, wide(56, 8))
    return final_product(jnp.stack([row_at, col_at]), turned, wide(32, 16), hi, lo)


def on_device(offsets, point_order, nugget, interp):
    row_at = lax.axis_index("row")
    col_at = lax.axis_index("col")
    corner = jnp.stack([row_at, col_at]).astype(jnp.float32)[:, None]
    order = point_order[0, 0]
    points = jnp.take(offsets[0, 0] + corner, order, axis=1)
    weights = jnp.take(nugget[0, 0], order)
    lines = jnp.concatenate([points.reshape(4, 128), weights.reshape(2, 128)])
    pack = jnp.concatenate([interp[0, 0], lines, jnp.zeros((2, 128), jnp.float32)])
    return root_phase(box_phase(pack), row_at, col_at)


def solution(mesh):
    in_specs = (
        P("row", "col", None, None),
        P("row", "col", None),
        P("row", "col", None),
        P("row", "col", None, None),
    )
    out_specs = P("row", "col")
    return jax.shard_map(
        on_device, mesh=mesh, in_specs=in_specs, out_specs=out_specs, check_vma=False
    )
```

profile of v0, /device:TPU:1, one launch (start us, length us, event | category | flops | bytes accessed | tf_op | source)
XLA Modules:
  0.0 250.4 jit_solution(685693398538120610)
XLA Ops:
  0.0 0.0 copy-start
  0.0 0.7 compare_select_fusion
  0.7 0.0 copy-done
  0.7 1.9 gather_fusion.1
  2.7 0.7 bitcast_select_fusion
  3.4 0.8 copy.15
  4.2 0.1 fusion
  4.3 0.7 gather_fusion
  5.0 0.1 copy.16
  5.1 0.1 pad.7.clone
  5.2 0.9 maximum_maximum_fusion.pack_ref
  6.1 82.8 %shard_map.46 = f32[128,4,8,128]{3,2,1,0:T(8,128)} custom-call(f32[136,128]{1,0:T(8,128)S(1)} %maximum_maximum_fusion.pack_ref), custom_call_target="tpu_custom_call" | custom-call | tf_op jit(solution)/shard_map/pallas_call | solution.py:372
  89.0 25.7 %all-to-all-start = ((f32[128,32,128]{2,1,0:T(8,128)}), f32[128,32,128]{2,1,0:T(8,128)}, u32[]{:S(2)}, u32[]{:S(2)}) async-start(f32[128,32,128]{2,1,0:T(8,128)} %bitcast.10), calls=%async_computation | async-start | bytes 4194304 | tf_op jit(solution)/shard_map/all_to_all | solution.py:656
  114.7 29.4 %all-to-all-done = f32[128,32,128]{2,1,0:T(8,128)} async-done(((f32[128,32,128]{2,1,0:T(8,128)}), f32[128,32,128]{2,1,0:T(8,128)}, u32[]{:S(2)}, u32[]{:S(2)}) %all-to-all-start) | async-done | bytes 2097184 | tf_op jit(solution)/shard_map/all_to_all | solution.py:656
  144.1 2.0 copy.17
  146.1 0.0 copy-start.1
  146.2 0.3 broadcast_in_dim.47.lead_ref
  146.5 0.9 copy-done.1
  147.4 63.9 %shard_map.47 = (bf16[1024,1024]{1,0:T(8,128)(2,1)S(1)}, bf16[1024,1024]{1,0:T(8,128)(2,1)S(1)}) custom-call(s32[1]{0:T(128)} %bitcast.14.flag_ref, f32[32,128,128]{2,1,0:T(8,128)} %bitcast.27, f32[8,2,128,128]{3,2,1,0:T(8,128)S(1)} %broadcast_in_dim.47.lead_ref), custom_call_target="tpu_custom_call" | custom-call | tf_op jit(solution)/shard_map/pallas_call | solution.py:550
  211.3 0.0 copy-start.3
  211.3 1.3 copy-done.3
  212.6 0.0 copy-start.4
  212.6 1.3 copy-done.4
  213.9 0.0 copy-start.2
  213.9 0.6 broadcast_in_dim.44.rows_ref
  214.5 1.0 copy-done.2
  215.5 34.9 %shard_map.48 = f32[2048,1024]{1,0:T(8,128)} custom-call(s32[2]{0:T(128)S(1)} %get-tuple-element.10.at_ref, f32[32,128,128]{2,1,0:T(8,128)S(1)} %bitcast.28, f32[16,2,128,128]{3,2,1,0:T(8,128)S(1)} %broadcast_in_dim.44.rows_ref, bf16[1024,1024]{1,0:T(8,128)(2,1)} %copy-done.3, bf16[1024,1024]{1,0:T(8,128)(2,1)} %copy-done.4), custom_call_target="tpu_custom_call" | custom-call | tf_op jit(solution)/shard_map/pallas_call | solution.py:635
  (13 shorter events, 0.1 us)
Async XLA Ops:
  0.0 0.7 copy-start
  89.0 55.1 %all-to-all-start = ((f32[128,32,128]{2,1,0:T(8,128)}), f32[128,32,128]{2,1,0:T(8,128)}, u32[]{:S(2)}, u32[]{:S(2)}) async-start(f32[128,32,128]{2,1,0:T(8,128)} %bitcast.10), calls=%async_computation | async-start | bytes 4194304 | tf_op jit(solution)/shard_map/all_to_all | solution.py:656
  146.1 1.3 copy-start.1
  211.3 1.3 copy-start.3
  212.6 1.3 copy-start.4
  213.9 1.6 copy-start.2
where the time goes:
time: 251 us; the launch traced here: 250 us
  Pallas kernels  182 us (73%)
  waiting for transfers between devices  29.4 us (12%)
  starting transfers between devices  25.7 us (10%)
  local copies, waits for them, and re-layouts  11.2 us (4%)
    pallas_call x1, Pallas kernels, box_phase(): pl.pallas_call(box_kernel, out_shape=jax.ShapeDtypeStruct((128, 4, 8, 128...  82.8 us
    pallas_call x1, Pallas kernels, root_solve(): pl.pallas_call(root_kernel, out_shape=[jax.ShapeDtypeStruct((SB, SB), jnp...  63.9 us
    pallas_call x1, Pallas kernels, final_product(): pl.pallas_call(final_kernel, grid=(steps + 1,), out_shape=jax.ShapeDtypeS...  34.9 us
    all_to_all x1, waiting for transfers between devices, root_phase(): lax.all_to_all(outgoing.reshape(128, 32, 128), ('row', 'col'), split_axis...  29.4 us
    all_to_all x1, starting transfers between devices, root_phase(): lax.all_to_all(outgoing.reshape(128, 32, 128), ('row', 'col'), split_axis...  25.7 us
    unnamed x11, local copies, waits for them, and re-layouts  5.35 us
  transfers between devices with their start and end apart: 1, of which 1 were waited for; matrix products, arithmetic and copies ran while one was open for 0% of the time, Pallas kernels for 0%

commit v1 on v0

--- a/solution.py
+++ b/solution.py
@@ -8,7 +8,6 @@
 SB = 1024
 
 
-kernel_amp = 0.015625
 kernel_len = 0.5
 
 
@@ -56,6 +55,12 @@
     return jnp.concatenate(us, 0), jnp.concatenate(ws, 0)
 
 
+def kappa(gap_x, gap_y):
+    square = gap_x * gap_x + gap_y * gap_y
+    distance = square * lax.rsqrt(jnp.maximum(square, 1e-36))
+    return jnp.exp2(distance * (-1.4426950408889634 / kernel_len) - 6.0)
+
+
 def split(x):
     hi = x.astype(jnp.bfloat16)
     return hi, (x - hi.astype(jnp.float32)).astype(jnp.bfloat16)
@@ -73,7 +78,7 @@
 NT = ((1,), (1,))
 
 
-def box_kernel(pack_ref, out_ref, near, ea, f, fs, g, mat, acc, tx, rx, fx, dd, ps, pr, ks, kr, xs, xr):
+def box_kernel(off_ref, order_ref, nug_ref, interp_ref, out_ref, pack_ref, near, ea, f, fs, g, mat, acc, tx, rx, fx, dd, ps, pr, ks, kr, xs, xr):
     row_at = lax.axis_index("row")
     col_at = lax.axis_index("col")
     row_count = lax.axis_size("row")
@@ -123,7 +128,8 @@
         return copy(pack_ref, near.at[8 - n], ps.at[n], pr.at[8 - n], a, b)
 
     def k_copy(n, e, a, b):
-        return copy(tx.at[e], rx.at[8 - n, e], ks.at[n, e], kr.at[8 - n, e], a, b)
+        source = tx if isinstance(e, int) else g.at[e]
+        return copy(source, rx.at[8 - n, e], ks.at[n, e], kr.at[8 - n, e], a, b)
 
     def x_copy(h, o):
         a, b = unslot(h)
@@ -140,12 +146,33 @@
         )
 
     neighbours(greet)
+    line = lax.broadcasted_iota(jnp.int32, (16, 256), 0)
+    plain = jnp.where(
+        line == 0,
+        off_ref[0:1] + row_at.astype(jnp.float32),
+        jnp.where(
+            line == 1,
+            off_ref[1:2] + col_at.astype(jnp.float32),
+            jnp.where(line == 2, nug_ref[...], 0.0),
+        ),
+    )
+    pick = lax.broadcasted_iota(jnp.int32, (256, 256), 0) == order_ref[...]
+    pick = jnp.where(pick, 1.0, 0.0).astype(jnp.bfloat16)
+    high = plain.astype(jnp.bfloat16)
+    middle, low = split(plain - high.astype(jnp.float32))
+    placed = mm(high, pick) + mm(middle, pick) + mm(low, pick)
+    level = lax.broadcasted_iota(jnp.int32, (8, 128), 0)
+    own = jnp.zeros((8, 128), jnp.float32)
+    for n in range(6):
+        half = slice(128 * (n % 2), 128 * (n % 2) + 128)
+        own = jnp.where(level == n, placed[n // 2 : n // 2 + 1, half], own)
+    pack_ref[0:128] = interp_ref[...]
+    pack_ref[128:136] = own
     tall = 1 + lax.min(row_at, 1) + lax.min(row_count - 1 - row_at, 1)
     wide = 1 + lax.min(col_at, 1) + lax.min(col_count - 1 - col_at, 1)
     pl.semaphore_wait(barrier, tall * wide - 1)
     neighbours(lambda n, a, b: pack_copy(n, a, b).start())
 
-    own = pack_ref[128:136]
     own_interp = split(pack_ref[0:128])
     my_colour = colour(0, 0)
     eye = lax.broadcasted_iota(jnp.int32, (128, 128), 0) == lax.broadcasted_iota(
@@ -160,8 +187,7 @@
             for t in range(2):
                 gap_row = where[:, s : s + 1] - own[t : t + 1]
                 gap_col = where[:, 2 + s : 3 + s] - own[2 + t : 3 + t]
-                square = gap_row * gap_row + gap_col * gap_col
-                block = kernel_amp * jnp.exp(-jnp.sqrt(square) / kernel_len)
+                block = kappa(gap_row, gap_col)
                 if here and s == t:
                     block = block + jnp.where(eye, own[4 + s : 5 + s], 0.0)
                 line.append(block)
@@ -180,27 +206,34 @@
     def stage(k):
         @pl.when(my_colour == k)
         def _():
-            tx[4] = factor128(mat[...])[1]
-
-            def outgoing(e):
-                ea_, eb_ = unslot(e)
-
-                def dispatch(n, a, b):
-                    @pl.when(near_pair(ea_ - a, eb_ - b))
+            tx[...] = factor128(mat[...])[1]
+            neighbours(lambda n, a, b: k_copy(n, 4, a, b).start())
+
+        def gather_terms(o):
+            oa, ob = unslot(o)
+
+            @pl.when(inside(oa, ob) & (colour(oa, ob) == k))
+            def _():
+                def term(e):
+                    ea_, eb_ = unslot(e)
+                    va, vb = oa + ea_, ob + eb_
+
+                    @pl.when((e != 4) & near_pair(va, vb) & inside(va, vb) & (colour(va, vb) < k))
                     def _():
-                        k_copy(n, e, a, b).start()
-
-                @pl.when(e == 4)
-                def _():
-                    neighbours(dispatch)
-
-                @pl.when((e != 4) & inside(ea_, eb_) & (colour(ea_, eb_) < k))
-                def _():
-                    tx[e] = dot3(split(tx[4]), split(g[e]), NT)
-                    neighbours(dispatch)
-
-            outgoing(4)
-            loop(lambda e: pl.when(e != 4)(lambda: outgoing(e)))
+                        right = split(f[(va + 1) * 3 + vb + 1])
+
+                        @pl.when(o == 4)
+                        def _():
+                            ea[o] -= dot3(split(g[e]), right, NN)
+
+                        @pl.when(o != 4)
+                        def _():
+                            k_copy(8 - o, e, -oa, -ob).wait_recv()
+                            ea[o] -= dot3(split(rx[o, e]), right, NN)
+
+                loop(term)
+
+        loop(gather_terms)
 
         def arrive(o):
             oa, ob = unslot(o)
@@ -209,40 +242,29 @@
             def _():
                 @pl.when(o == 4)
                 def _():
-                    acc[...] = dot3(split(tx[4]), split(ea[4]), NN)
+                    acc[...] = dot3(split(tx[...]), split(ea[4]), NN)
 
                 @pl.when(o != 4)
                 def _():
                     k_copy(8 - o, 4, -oa, -ob).wait_recv()
                     acc[...] = dot3(split(rx[o, 4]), split(ea[o]), NN)
 
-                def term(e):
-                    ea_, eb_ = unslot(e)
-                    va, vb = oa + ea_, ob + eb_
-
-                    @pl.when((e != 4) & near_pair(va, vb) & inside(va, vb) & (colour(va, vb) < k))
-                    def _():
-                        right = split(f[(va + 1) * 3 + vb + 1])
-
-                        @pl.when(o == 4)
-                        def _():
-                            acc[...] -= dot3(split(tx[e]), right, NN)
-
-                        @pl.when(o != 4)
-                        def _():
-                            k_copy(8 - o, e, -oa, -ob).wait_recv()
-                            acc[...] -= dot3(split(rx[o, e]), right, NN)
-
-                loop(term)
                 f[o] = acc[...]
                 fs[o] = acc[:, :128]
 
                 @pl.when(my_colour > k)
                 def _():
                     new = acc[:, 128:] - dot3(split(acc[:, :128]), own_interp, NN)
-                    g[o] = new
-                    new2 = split(new)
-                    mat[...] -= dot3(new2, new2, TN)
+                    flip = new.T
+                    g[o] = flip
+                    mat[...] -= dot3(split(flip), split(new), NN)
+
+                    def early(n, a, b):
+                        @pl.when(near_pair(oa - a, ob - b))
+                        def _():
+                            k_copy(n, o, a, b).start()
+
+                    neighbours(early)
 
                 def forward(h):
                     ha, hb = unslot(h)
@@ -367,14 +389,15 @@
     loop(finish_x, 5, 9)
 
 
-def box_phase(pack):
+def box_phase(off, order, nug, interp):
     block = (128, 128)
     return pl.pallas_call(
         box_kernel,
         out_shape=jax.ShapeDtypeStruct((128, 4, 8, 128), jnp.float32),
-        in_specs=[pl.BlockSpec(memory_space=pltpu.VMEM)],
+        in_specs=[pl.BlockSpec(memory_space=pltpu.VMEM)] * 4,
         out_specs=pl.BlockSpec(memory_space=pltpu.VMEM),
         scratch_shapes=[
+            pltpu.VMEM((136, 128), jnp.float32),
             pltpu.VMEM((9, 136, 128), jnp.float32),
             pltpu.VMEM((9, 128, 256), jnp.float32),
             pltpu.VMEM((9, 128, 256), jnp.float32),
@@ -382,7 +405,7 @@
             pltpu.VMEM((9,) + block, jnp.float32),
             pltpu.VMEM(block, jnp.float32),
             pltpu.VMEM((128, 256), jnp.float32),
-            pltpu.VMEM((9,) + block, jnp.float32),
+            pltpu.VMEM(block, jnp.float32),
             pltpu.VMEM((9, 9) + block, jnp.float32),
             pltpu.VMEM((4, 9) + block, jnp.float32),
             pltpu.VMEM((9,) + block, jnp.float32),
@@ -396,7 +419,7 @@
         compiler_params=pltpu.CompilerParams(
             collective_id=0, has_side_effects=True, vmem_limit_bytes=40 * 2**20
         ),
-    )(pack)
+    )(off, order, nug, interp)
 
 
 def cat_right(x):
@@ -425,9 +448,7 @@
 def root_block(row_x, row_y, col_x, col_y, lines):
     gap_x = row_x - col_x
     gap_y = row_y - col_y
-    square = gap_x * gap_x + gap_y * gap_y
-    distance = square * lax.rsqrt(jnp.maximum(square, 1e-36))
-    value = jnp.exp2(distance * (-1.4426950408889634 / kernel_len) - 6.0)
+    value = kappa(gap_x, gap_y)
     gap = apart()
     extra = jnp.zeros((128, 128), jnp.float32)
     for n in range(9):
@@ -569,7 +590,7 @@
     )(flag, turned, lead)
 
 
-def final_kernel(at_ref, turned, rows_ref, hi_ref, lo_ref, out_ref, tab, buffer):
+def final_kernel(at_ref, turned, rows_ref, hi_ref, lo_ref, out_ref, tab, buf_a, buf_b):
     rows, cols = out_ref.shape
     s = pl.program_id(0)
 
@@ -595,37 +616,49 @@
             lines,
         )
 
-    ahead = lax.min(s, pl.num_programs(0) - 2)
-    now = lax.max(s - 1, 0)
-    slot, other = s % 2, (s + 1) % 2
-    first = at_ref[0] * (rows * (pl.num_programs(0) - 1)) + now * rows
-    start = at_ref[1] * cols
+    def fill(buffer, block, l):
+        for half in range(2):
+            hi, lo = split(piece(1, 2 * block + half, l))
+            buffer[0, 128 * half : 128 * half + 128, 128 * l : 128 * l + 128] = hi
+            buffer[1, 128 * half : 128 * half + 128, 128 * l : 128 * l + 128] = lo
+
+    @pl.when(s == 0)
+    def _():
+        for l in range(8):
+            fill(buf_a, 0, l)
+
+    blocks = pl.num_programs(0) * 2
     row = lax.broadcasted_iota(jnp.int32, (128, 128), 0)
     col = lax.broadcasted_iota(jnp.int32, (128, 128), 1)
-    for c in range(cols // 256):
-        some = slice(c * 256, c * 256 + 256)
-        for half in range(2):
+    start = at_ref[1] * cols
+    for turn in range(2):
+        now = 2 * s + turn
+        mine, other = (buf_a, buf_b) if turn == 0 else (buf_b, buf_a)
+        first = (at_ref[0] * blocks + now) * 256
+        ahead = lax.min(now + 1, blocks - 1)
+        for c in range(cols // 256):
+            some = slice(c * 256, c * 256 + 256)
+            hi, lo = hi_ref[:, some], lo_ref[:, some]
+            x_hi, x_lo = mine[0], mine[1]
+            product = mm(x_hi, lo) + mm(x_lo, hi) + mm(x_hi, hi)
             for l in (2 * c, 2 * c + 1):
-                hi, lo = split(piece(1, 2 * ahead + half, l))
-                buffer[slot, 0, 128 * half : 128 * half + 128, 128 * l : 128 * l + 128] = hi
-                buffer[slot, 1, 128 * half : 128 * half + 128, 128 * l : 128 * l + 128] = lo
-        x_hi, x_lo = buffer[other, 0], buffer[other, 1]
-        hi, lo = hi_ref[:, some], lo_ref[:, some]
-        product = mm(x_hi, lo) + mm(x_lo, hi) + mm(x_hi, hi)
-        for half in range(2):
-            for l in (2 * c, 2 * c + 1):
-                base = piece(0, 2 * now + half, l)
-                part = product[128 * half : 128 * half + 128, 128 * (l % 2) : 128 * (l % 2) + 128]
-                value = jnp.where(at_ref[1] == 0, 0.0, base) - part
-                here = first + 128 * half + row
-                there = start + 128 * l + col
-                out_ref[128 * half : 128 * half + 128, 128 * l : 128 * l + 128] = jnp.where(
-                    (here < SB) & (there > here), 0.0, value
-                )
+                fill(other, ahead, l)
+                for half in range(2):
+                    base = piece(0, 2 * now + half, l)
+                    part = product[
+                        128 * half : 128 * half + 128, 128 * (l % 2) : 128 * (l % 2) + 128
+                    ]
+                    value = jnp.where(at_ref[1] == 0, 0.0, base) - part
+                    here = first + 128 * half + row
+                    there = start + 128 * l + col
+                    place = 256 * turn + 128 * half
+                    out_ref[place : place + 128, 128 * l : 128 * l + 128] = jnp.where(
+                        (here < SB) & (there > here), 0.0, value
+                    )
 
 
 def final_product(at, turned, rows_wide, hi, lo):
-    block = 256
+    block = 512
     steps = 2048 // block
     cols = hi.shape[1]
 
@@ -634,7 +667,7 @@
 
     return pl.pallas_call(
         final_kernel,
-        grid=(steps + 1,),
+        grid=(steps,),
         out_shape=jax.ShapeDtypeStruct((steps * block, cols), jnp.float32),
         in_specs=[
             pl.BlockSpec(memory_space=pltpu.SMEM),
@@ -643,10 +676,11 @@
             whole(hi),
             whole(lo),
         ],
-        out_specs=pl.BlockSpec((block, cols), lambda i: (lax.max(i - 1, 0), 0)),
+        out_specs=pl.BlockSpec((block, cols), lambda i: (i, 0)),
         scratch_shapes=[
             pltpu.VMEM((2, 8, 9, 16, 128), jnp.float32),
-            pltpu.VMEM((2, 2, block, SB), jnp.bfloat16),
+            pltpu.VMEM((2, block // 2, SB), jnp.bfloat16),
+            pltpu.VMEM((2, block // 2, SB), jnp.bfloat16),
         ],
         compiler_params=pltpu.CompilerParams(vmem_limit_bytes=48 * 2**20),
     )(at, turned, rows_wide, hi, lo)
@@ -668,15 +702,8 @@
 
 
 def on_device(offsets, point_order, nugget, interp):
-    row_at = lax.axis_index("row")
-    col_at = lax.axis_index("col")
-    corner = jnp.stack([row_at, col_at]).astype(jnp.float32)[:, None]
-    order = point_order[0, 0]
-    points = jnp.take(offsets[0, 0] + corner, order, axis=1)
-    weights = jnp.take(nugget[0, 0], order)
-    lines = jnp.concatenate([points.reshape(4, 128), weights.reshape(2, 128)])
-    pack = jnp.concatenate([interp[0, 0], lines, jnp.zeros((2, 128), jnp.float32)])
-    return root_phase(box_phase(pack), row_at, col_at)
+    outgoing = box_phase(offsets[0, 0], point_order[0], nugget[0], interp[0, 0])
+    return root_phase(outgoing, lax.axis_index("row"), lax.axis_index("col"))
 
 
 def solution(mesh):

time: 251 us -> 228 us (0.908)
  Pallas kernels: 182 us -> 164 us
    pallas_call x1, Pallas kernels: 82.8 us -> 66.8 us  [box_phase(): pl.pallas_call(box_kernel, out_shape=jax.ShapeDtypeStruct((128, 4, 8, 128...]
    gather x4 -> x0, local copies, waits for them, and re-layouts: 2.77 us -> none  [the longest x1 1.94 us: on_device(): weights = jnp.take(nugget[0, 0], order)]
    unnamed x11 -> x16, local copies, waits for them, and re-layouts: 5.35 us -> 7.41 us
where the time goes in v1:
time: 228 us; the launch traced here: 227 us
  Pallas kernels  164 us (72%)
  waiting for transfers between devices  29.3 us (13%)
  starting transfers between devices  23.7 us (10%)
  local copies, waits for them, and re-layouts  10.4 us (5%)
    pallas_call x1, Pallas kernels, box_phase(): pl.pallas_call(box_kernel, out_shape=jax.ShapeDtypeStruct((128, 4, 8, 128...  66.8 us
    pallas_call x1, Pallas kernels, root_solve(): pl.pallas_call(root_kernel, out_shape=[jax.ShapeDtypeStruct((SB, SB), jnp...  63.8 us
    pallas_call x1, Pallas kernels, final_product(): pl.pallas_call(final_kernel, grid=(steps,), out_shape=jax.ShapeDtypeStruc...  33.3 us
    all_to_all x1, waiting for transfers between devices, root_phase(): lax.all_to_all(outgoing.reshape(128, 32, 128), ('row', 'col'), split_axis...  29.3 us
    all_to_all x1, starting transfers between devices, root_phase(): lax.all_to_all(outgoing.reshape(128, 32, 128), ('row', 'col'), split_axis...  23.7 us
    unnamed x16, local copies, waits for them, and re-layouts  7.41 us
  transfers between devices with their start and end apart: 1, of which 1 were waited for; matrix products, arithmetic and copies ran while one was open for 0% of the time, Pallas kernels for 0%

profile of v1, /device:TPU:1, one launch (start us, length us, event | category | flops | bytes accessed | tf_op | source)
XLA Modules:
  0.0 227.4 jit_solution(2096049045372251064)
XLA Ops:
  0.0 0.0 copy-start.4
  0.0 0.8 copy-done.4
  0.8 0.0 copy-start.5
  0.8 0.7 copy-done.5
  1.5 0.0 copy-start.6
  1.5 0.7 copy-done.6
  2.2 0.0 copy-start.7
  2.2 0.7 copy-done.7
  2.9 66.8 %shard_map.46 = f32[128,4,8,128]{3,2,1,0:T(8,128)} custom-call(f32[2,256]{1,0:T(2,128)S(1)} %bitcast.22, s32[1,256]{1,0:T(1,128)S(1)} %bitcast.23, f32[1,256]{1,0:T(1,128)S(1)} %bitcast.24, f32[128,128]{1,0:T(8,128)S(1)} %bitcast.21), custom_call_target="tpu_custom_call" | custom-call | tf_op jit(solution)/shard_map/pallas_call | solution.py:394
  69.7 23.7 %all-to-all-start = ((f32[128,32,128]{2,1,0:T(8,128)}), f32[128,32,128]{2,1,0:T(8,128)}, u32[]{:S(2)}, u32[]{:S(2)}) async-start(f32[128,32,128]{2,1,0:T(8,128)} %bitcast.6), calls=%async_computation | async-start | bytes 4194304 | tf_op jit(solution)/shard_map/all_to_all | solution.py:690
  93.4 0.1 pad_add_fusion.at_ref
  93.4 29.3 %all-to-all-done = f32[128,32,128]{2,1,0:T(8,128)} async-done(((f32[128,32,128]{2,1,0:T(8,128)}), f32[128,32,128]{2,1,0:T(8,128)}, u32[]{:S(2)}, u32[]{:S(2)}) %all-to-all-start) | async-done | bytes 2097184 | tf_op jit(solution)/shard_map/all_to_all | solution.py:690
  122.7 2.0 copy.8
  124.8 0.0 copy-start
  124.8 0.3 broadcast_in_dim.20.lead_ref
  125.2 0.9 copy-done
  126.1 63.8 %shard_map.47 = (bf16[1024,1024]{1,0:T(8,128)(2,1)S(1)}, bf16[1024,1024]{1,0:T(8,128)(2,1)S(1)}) custom-call(s32[1]{0:T(128)} %bitcast.10.flag_ref, f32[32,128,128]{2,1,0:T(8,128)} %bitcast.19, f32[8,2,128,128]{3,2,1,0:T(8,128)S(1)} %broadcast_in_dim.20.lead_ref), custom_call_target="tpu_custom_call" | custom-call | tf_op jit(solution)/shard_map/pallas_call | solution.py:571
  189.9 0.0 copy-start.2
  189.9 1.3 copy-done.2
  191.2 0.0 copy-start.3
  191.2 1.3 copy-done.3
  192.5 0.0 copy-start.1
  192.5 0.6 broadcast_in_dim.8.rows_ref
  193.1 1.0 copy-done.1
  194.1 33.3 %shard_map.48 = f32[2048,1024]{1,0:T(8,128)} custom-call(s32[2]{0:T(128)S(1)} %pad_add_fusion.at_ref, f32[32,128,128]{2,1,0:T(8,128)S(1)} %bitcast.20, f32[16,2,128,128]{3,2,1,0:T(8,128)S(1)} %broadcast_in_dim.8.rows_ref, bf16[1024,1024]{1,0:T(8,128)(2,1)} %copy-done.2, bf16[1024,1024]{1,0:T(8,128)(2,1)} %copy-done.3), custom_call_target="tpu_custom_call" | custom-call | tf_op jit(solution)/shard_map/pallas_call | solution.py:668
  (6 shorter events, 0.0 us)
Async XLA Ops:
  0.0 0.8 copy-start.4
  0.8 0.7 copy-start.5
  1.5 0.7 copy-start.6
  2.2 0.7 copy-start.7
  69.7 53.0 %all-to-all-start = ((f32[128,32,128]{2,1,0:T(8,128)}), f32[128,32,128]{2,1,0:T(8,128)}, u32[]{:S(2)}, u32[]{:S(2)}) async-start(f32[128,32,128]{2,1,0:T(8,128)} %bitcast.6), calls=%async_computation | async-start | bytes 4194304 | tf_op jit(solution)/shard_map/all_to_all | solution.py:690
  124.8 1.3 copy-start
  189.9 1.3 copy-start.2
  191.2 1.3 copy-start.3
  192.5 1.6 copy-start.1

commit v2 on v1

--- a/solution.py
+++ b/solution.py
@@ -460,7 +460,27 @@
     return pltpu.roll(line, -OFFSETS[n] % 128, 1) if n > 4 else line
 
 
-def root_kernel(flag_ref, turned, lead_ref, hi_ref, lo_ref, work, diag, wcur, left, right, wt, tab):
+def tail_kernel(
+    at_ref,
+    turned,
+    lead_ref,
+    rows_ref,
+    out_ref,
+    work,
+    diag,
+    wcur,
+    left,
+    right,
+    wt,
+    z_hi,
+    z_lo,
+    x_hi,
+    x_lo,
+    base,
+    tab,
+    table,
+    sems,
+):
     count = SB // 128
     width = 3 * SB
     chunk = 256
@@ -476,20 +496,38 @@
             line = turned[16 + l, place : place + 8] if n < 8 else turned[24 + l, 0:8]
             tab[0, l, n] = shifted_line(line, n)
             tab[1, l, n] = shifted_line(turned[24 + l, 8 + 8 * n : 16 + 8 * n], n)
+            place = 16 * (n - 1)
+            line = turned[l, place : place + 16] if n else turned[8 + l, 0:16]
+            table[0, l, n] = shifted_line(line, n)
+            place = 16 * n + 16
+            if n < 7:
+                line = turned[8 + l, place : place + 16]
+            else:
+                line = turned[16 + l, place - 128 : place - 112]
+            table[1, l, n] = shifted_line(line, n)
+
+    def piece(values, wide, which, k, l):
+        place = 48 + 8 * which + l
+        return root_block(
+            wide[k, 0],
+            wide[k, 1],
+            turned[16, place : place + 1],
+            turned[18, place : place + 1],
+            [values[which, l, n, pl.ds(k, 1)] for n in range(9)],
+        )
 
     def assemble(k, _):
         for l in range(8):
-            for which in range(2):
-                place = 48 + 8 * which + l
-                lines = [tab[which, l, n, pl.ds(k, 1)] for n in range(9)]
-                start = SB * (1 - which) + 128 * l
-                work[rows_of(k), start : start + 128] = root_block(
-                    lead_ref[k, 0],
-                    lead_ref[k, 1],
-                    turned[16, place : place + 1],
-                    turned[18, place : place + 1],
-                    lines,
-                )
+            work[rows_of(k), SB + 128 * l : SB + 128 * l + 128] = piece(tab, lead_ref, 0, k, l)
+
+            @pl.when(k <= l)
+            def _():
+                work[rows_of(k), 128 * l : 128 * l + 128] = piece(tab, lead_ref, 1, k, l)
+
+            @pl.when(k > l)
+            def _():
+                work[rows_of(k), 128 * l : 128 * l + 128] = jnp.zeros((128, 128), jnp.float32)
+
         return 0
 
     lax.fori_loop(0, count, assemble, 0)
@@ -498,6 +536,14 @@
     work[SB:] = jnp.zeros((128, width), jnp.float32)
     diag[...] = work[:128, :128]
     wcur[...] = jnp.zeros((128, 384), jnp.bfloat16)
+
+    def build(k):
+        for l in range(8):
+            cols = slice(128 * l, 128 * l + 128)
+            hi, lo = split(piece(table, rows_ref, 1, k, l))
+            x_hi[rows_of(k), cols] = hi
+            x_lo[rows_of(k), cols] = lo
+            base[rows_of(k), cols] = piece(table, rows_ref, 0, k, l)
 
     def scale(p):
         here = rows_of(p)
@@ -518,6 +564,8 @@
         for c in range(width // chunk):
             cols = slice(c * chunk, c * chunk + chunk)
             work[:SB, cols] -= mm(left[...], right[:, cols])
+        build(2 * i)
+        build(2 * i + 1)
         w = factor128(diag[...])[1]
         wcur[...] = cat_left(w)
         here, after = rows_of(i), rows_of(i + 1)
@@ -534,14 +582,14 @@
     def flip(i, _):
         here = rows_of(i)
 
-        @pl.when(flag_ref[0] == 1)
+        @pl.when(at_ref[1] == 0)
         def _():
             work[here, SB : 2 * SB] = jnp.where(col == row + 128 * i, -1.0, 0.0)
 
         hi, lo = split(work[here, SB : 2 * SB])
         right[0:128, :SB] = hi
-        hi_ref[here] = hi
-        lo_ref[here] = lo
+        z_hi[here] = hi
+        z_lo[here] = lo
         for j in range(count):
             hi, lo = split(work[here, 2 * SB + 128 * j : 2 * SB + 128 * j + 128].T)
             there = slice(128 * j, 128 * j + 128)
@@ -552,7 +600,7 @@
     lax.fori_loop(0, count, flip, 0)
     for c in range(SB // chunk):
         cols = slice(c * chunk, c * chunk + chunk)
-        y_hi, y_lo = hi_ref[:, cols], lo_ref[:, cols]
+        y_hi, y_lo = z_hi[:, cols], z_lo[:, cols]
         for m in range(4):
             some = slice(m * 256, m * 256 + 256)
             deep = slice(m * 256, SB)
@@ -563,20 +611,40 @@
         for m in range(4):
             some = slice(m * 256, m * 256 + 256)
             hi, lo = split(work[some, cols])
-            hi_ref[some, cols] = hi
-            lo_ref[some, cols] = lo
-
-
-def root_solve(flag, turned, lead):
+            z_hi[some, cols] = hi
+            z_lo[some, cols] = lo
+
+    tall = 512
+
+    def product(r, _):
+        here = pl.ds(pl.multiple_of(r * tall, tall), tall)
+        for c in range(SB // chunk):
+            cols = slice(c * chunk, c * chunk + chunk)
+            part = (
+                mm(x_hi[here], z_lo[:, cols])
+                + mm(x_lo[here], z_hi[:, cols])
+                + mm(x_hi[here], z_hi[:, cols])
+            )
+            value = jnp.where(at_ref[1] == 0, 0.0, base[here, cols]) - part
+            down = (at_ref[0] * 4 + r) * tall + lax.broadcasted_iota(jnp.int32, value.shape, 0)
+            over = at_ref[1] * SB + c * chunk + lax.broadcasted_iota(jnp.int32, value.shape, 1)
+            base[here, cols] = jnp.where((down < SB) & (over > down), 0.0, value)
+        pltpu.make_async_copy(base.at[here], out_ref.at[here], sems.at[r]).start()
+        return 0
+
+    lax.fori_loop(0, 4, product, 0)
+    for r in range(4):
+        here = slice(r * tall, r * tall + tall)
+        pltpu.make_async_copy(base.at[here], out_ref.at[here], sems.at[r]).wait()
+
+
+def tail_solve(at, turned, lead, rows_wide):
+    vmem = pl.BlockSpec(memory_space=pltpu.VMEM)
     return pl.pallas_call(
-        root_kernel,
-        out_shape=[jax.ShapeDtypeStruct((SB, SB), jnp.bfloat16)] * 2,
-        in_specs=[
-            pl.BlockSpec(memory_space=pltpu.SMEM),
-            pl.BlockSpec(memory_space=pltpu.VMEM),
-            pl.BlockSpec(memory_space=pltpu.VMEM),
-        ],
-        out_specs=[pl.BlockSpec(memory_space=pltpu.VMEM)] * 2,
+        tail_kernel,
+        out_shape=jax.ShapeDtypeStruct((2048, SB), jnp.float32),
+        in_specs=[pl.BlockSpec(memory_space=pltpu.SMEM), vmem, vmem, vmem],
+        out_specs=pl.BlockSpec(memory_space=pl.ANY),
         scratch_shapes=[
             pltpu.VMEM((SB + 128, 3 * SB), jnp.float32),
             pltpu.VMEM((128, 128), jnp.float32),
@@ -584,106 +652,17 @@
             pltpu.VMEM((SB, 384), jnp.bfloat16),
             pltpu.VMEM((384, 3 * SB), jnp.bfloat16),
             pltpu.VMEM((2, SB, SB), jnp.bfloat16),
+            pltpu.VMEM((SB, SB), jnp.bfloat16),
+            pltpu.VMEM((SB, SB), jnp.bfloat16),
+            pltpu.VMEM((2048, SB), jnp.bfloat16),
+            pltpu.VMEM((2048, SB), jnp.bfloat16),
+            pltpu.VMEM((2048, SB), jnp.float32),
             pltpu.VMEM((2, 8, 9, 8, 128), jnp.float32),
+            pltpu.VMEM((2, 8, 9, 16, 128), jnp.float32),
+            pltpu.SemaphoreType.DMA((4,)),
         ],
-        compiler_params=pltpu.CompilerParams(vmem_limit_bytes=48 * 2**20),
-    )(flag, turned, lead)
-
-
-def final_kernel(at_ref, turned, rows_ref, hi_ref, lo_ref, out_ref, tab, buf_a, buf_b):
-    rows, cols = out_ref.shape
-    s = pl.program_id(0)
-
-    @pl.when(s == 0)
-    def _():
-        for l in range(8):
-            for n in range(9):
-                place = 16 * (n - 1)
-                line = turned[l, place : place + 16] if n else turned[8 + l, 0:16]
-                tab[0, l, n] = shifted_line(line, n)
-                place = 16 * n + 16
-                line = turned[8 + l, place : place + 16] if n < 7 else turned[16 + l, place - 128 : place - 112]
-                tab[1, l, n] = shifted_line(line, n)
-
-    def piece(which, k, l):
-        place = 48 + 8 * which + l
-        lines = [tab[which, l, n, pl.ds(k, 1)] for n in range(9)]
-        return root_block(
-            rows_ref[k, 0],
-            rows_ref[k, 1],
-            turned[16, place : place + 1],
-            turned[18, place : place + 1],
-            lines,
-        )
-
-    def fill(buffer, block, l):
-        for half in range(2):
-            hi, lo = split(piece(1, 2 * block + half, l))
-            buffer[0, 128 * half : 128 * half + 128, 128 * l : 128 * l + 128] = hi
-            buffer[1, 128 * half : 128 * half + 128, 128 * l : 128 * l + 128] = lo
-
-    @pl.when(s == 0)
-    def _():
-        for l in range(8):
-            fill(buf_a, 0, l)
-
-    blocks = pl.num_programs(0) * 2
-    row = lax.broadcasted_iota(jnp.int32, (128, 128), 0)
-    col = lax.broadcasted_iota(jnp.int32, (128, 128), 1)
-    start = at_ref[1] * cols
-    for turn in range(2):
-        now = 2 * s + turn
-        mine, other = (buf_a, buf_b) if turn == 0 else (buf_b, buf_a)
-        first = (at_ref[0] * blocks + now) * 256
-        ahead = lax.min(now + 1, blocks - 1)
-        for c in range(cols // 256):
-            some = slice(c * 256, c * 256 + 256)
-            hi, lo = hi_ref[:, some], lo_ref[:, some]
-            x_hi, x_lo = mine[0], mine[1]
-            product = mm(x_hi, lo) + mm(x_lo, hi) + mm(x_hi, hi)
-            for l in (2 * c, 2 * c + 1):
-                fill(other, ahead, l)
-                for half in range(2):
-                    base = piece(0, 2 * now + half, l)
-                    part = product[
-                        128 * half : 128 * half + 128, 128 * (l % 2) : 128 * (l % 2) + 128
-                    ]
-                    value = jnp.where(at_ref[1] == 0, 0.0, base) - part
-                    here = first + 128 * half + row
-                    there = start + 128 * l + col
-                    place = 256 * turn + 128 * half
-                    out_ref[place : place + 128, 128 * l : 128 * l + 128] = jnp.where(
-                        (here < SB) & (there > here), 0.0, value
-                    )
-
-
-def final_product(at, turned, rows_wide, hi, lo):
-    block = 512
-    steps = 2048 // block
-    cols = hi.shape[1]
-
-    def whole(x):
-        return pl.BlockSpec(x.shape, lambda i: (0,) * x.ndim)
-
-    return pl.pallas_call(
-        final_kernel,
-        grid=(steps,),
-        out_shape=jax.ShapeDtypeStruct((steps * block, cols), jnp.float32),
-        in_specs=[
-            pl.BlockSpec(memory_space=pltpu.SMEM),
-            whole(turned),
-            whole(rows_wide),
-            whole(hi),
-            whole(lo),
-        ],
-        out_specs=pl.BlockSpec((block, cols), lambda i: (i, 0)),
-        scratch_shapes=[
-            pltpu.VMEM((2, 8, 9, 16, 128), jnp.float32),
-            pltpu.VMEM((2, block // 2, SB), jnp.bfloat16),
-            pltpu.VMEM((2, block // 2, SB), jnp.bfloat16),
-        ],
-        compiler_params=pltpu.CompilerParams(vmem_limit_bytes=48 * 2**20),
-    )(at, turned, rows_wide, hi, lo)
+        compiler_params=pltpu.CompilerParams(vmem_limit_bytes=60 * 2**20),
+    )(at, turned, lead, rows_wide)
 
 
 def root_phase(outgoing, row_at, col_at):
@@ -696,9 +675,7 @@
         part = jnp.stack([turned[16, start : start + size], turned[18, start : start + size]], axis=1)
         return jnp.broadcast_to(part[:, :, :, None], part.shape + (128,))
 
-    flag = (col_at == 0).astype(jnp.int32)
-    hi, lo = root_solve(flag[None], turned, wide(56, 8))
-    return final_product(jnp.stack([row_at, col_at]), turned, wide(32, 16), hi, lo)
+    return tail_solve(jnp.stack([row_at, col_at]), turned, wide(56, 8), wide(32, 16))
 
 
 def on_device(offsets, point_order, nugget, interp):

time: 228 us -> 226 us (level)
    unnamed x16 -> x10, local copies, waits for them, and re-layouts: 7.41 us -> 2.88 us
    broadcast_in_dim x2, local copies, waits for them, and re-layouts: 0.92 us -> 3.55 us  [wide(): return jnp.broadcast_to(part[:, :, :, None], part.shape + (128,))]
    pallas_call x2 -> x1, Pallas kernels: 97.1 us -> 97.4 us  [tail_solve(): pl.pallas_call(tail_kernel, out_shape=jax.ShapeDtypeStruct((2048, SB), jn...]
where the time goes in v2:
time: 226 us
  Pallas kernels  164 us (73%)
  waiting for transfers between devices  28.7 us (13%)
  starting transfers between devices  23.7 us (10%)
  local copies, waits for them, and re-layouts  8.46 us (4%)
    pallas_call x1, Pallas kernels, tail_solve(): pl.pallas_call(tail_kernel, out_shape=jax.ShapeDtypeStruct((2048, SB), jn...  97.4 us
    pallas_call x1, Pallas kernels, box_phase(): pl.pallas_call(box_kernel, out_shape=jax.ShapeDtypeStruct((128, 4, 8, 128...  66.8 us
    all_to_all x1, waiting for transfers between devices, root_phase(): lax.all_to_all(outgoing.reshape(128, 32, 128), ('row', 'col'), split_axis...  28.7 us
    all_to_all x1, starting transfers between devices, root_phase(): lax.all_to_all(outgoing.reshape(128, 32, 128), ('row', 'col'), split_axis...  23.7 us
  transfers between devices with their start and end apart: 1, of which 1 were waited for; matrix products, arithmetic and copies ran while one was open for 0% of the time, Pallas kernels for 0%

profile of v2, /device:TPU:1, one launch (start us, length us, event | category | flops | bytes accessed | tf_op | source)
XLA Modules:
  0.0 226.0 jit_solution(14214113626685242676)
XLA Ops:
  0.0 0.0 copy-start
  0.0 0.8 copy-done
  0.8 0.0 copy-start.1
  0.8 0.7 copy-done.1
  1.5 0.0 copy-start.2
  1.5 0.7 copy-done.2
  2.2 0.0 copy-start.3
  2.2 0.7 copy-done.3
  2.9 66.8 %shard_map.46 = f32[128,4,8,128]{3,2,1,0:T(8,128)} custom-call(f32[2,256]{1,0:T(2,128)S(1)} %bitcast.17, s32[1,256]{1,0:T(1,128)S(1)} %bitcast.18, f32[1,256]{1,0:T(1,128)S(1)} %bitcast.19, f32[128,128]{1,0:T(8,128)S(1)} %bitcast.16), custom_call_target="tpu_custom_call" | custom-call | tf_op jit(solution)/shard_map/pallas_call | solution.py:394
  69.7 23.7 %all-to-all-start = ((f32[128,32,128]{2,1,0:T(8,128)}), f32[128,32,128]{2,1,0:T(8,128)}, u32[]{:S(2)}, u32[]{:S(2)}) async-start(f32[128,32,128]{2,1,0:T(8,128)} %bitcast.6), calls=%async_computation | async-start | bytes 4194304 | tf_op jit(solution)/shard_map/all_to_all | solution.py:669
  93.4 0.7 pad_add_fusion.at_ref
  94.0 28.7 %all-to-all-done = f32[128,32,128]{2,1,0:T(8,128)} async-done(((f32[128,32,128]{2,1,0:T(8,128)}), f32[128,32,128]{2,1,0:T(8,128)}, u32[]{:S(2)}, u32[]{:S(2)}) %all-to-all-start) | async-done | bytes 2097184 | tf_op jit(solution)/shard_map/all_to_all | solution.py:669
  122.7 2.0 copy.8
  124.7 0.0 copy-start.4
  124.8 1.6 broadcast_in_dim.4.lead_ref
  126.5 1.9 broadcast_in_dim.5.rows_ref
  128.4 0.0 copy-done.4
  128.4 97.4 %shard_map.47 = f32[2048,1024]{1,0:T(8,128)} custom-call(s32[2]{0:T(128)} %pad_add_fusion.at_ref, f32[32,128,128]{2,1,0:T(8,128)} %bitcast.22, f32[8,2,128,128]{3,2,1,0:T(8,128)} %broadcast_in_dim.4.lead_ref, f32[16,2,128,128]{3,2,1,0:T(8,128)} %broadcast_in_dim.5.rows_ref), custom_call_target="tpu_custom_call" | custom-call | tf_op jit(solution)/shard_map/pallas_call | solution.py:643
  (6 shorter events, 0.0 us)
Async XLA Ops:
  0.0 0.8 copy-start
  0.8 0.7 copy-start.1
  1.5 0.7 copy-start.2
  2.2 0.7 copy-start.3
  69.7 53.0 %all-to-all-start = ((f32[128,32,128]{2,1,0:T(8,128)}), f32[128,32,128]{2,1,0:T(8,128)}, u32[]{:S(2)}, u32[]{:S(2)}) async-start(f32[128,32,128]{2,1,0:T(8,128)} %bitcast.6), calls=%async_computation | async-start | bytes 4194304 | tf_op jit(solution)/shard_map/all_to_all | solution.py:669
  124.7 3.6 %copy-start.4 = (f32[128,32,128]{0,2,1:T(8,128)}, f32[128,32,128]{0,2,1:T(8,128)S(1)}, u32[]{:S(2)}) copy-start(f32[128,32,128]{0,2,1:T(8,128)S(1)} %copy.8) | copy-start | bytes 6291460

commit v3 on v2

--- a/solution.py
+++ b/solution.py
@@ -11,7 +11,7 @@
 kernel_len = 0.5
 
 
-def factor128(a):
+def factor128(a, side=None):
     n = a.shape[0]
     G = n // 8
     rows = [a[8*g:8*g+8] for g in range(G)]
@@ -39,6 +39,8 @@
             qw = qw - m * pw
             for v in range(t + 1, 8):
                 cols[v] = cols[v] - m * srow(cols[v], t)
+        if side is not None:
+            side(p, jnp.minimum(jnp.abs(dv[0:1]), 0.0))
         r = lax.rsqrt(dv)
         us.append(jnp.where(lane >= sub + 8*p, u * r, 0.0))
         ws.append(uw * r)
@@ -127,8 +129,8 @@
     def pack_copy(n, a, b):
         return copy(pack_ref, near.at[8 - n], ps.at[n], pr.at[8 - n], a, b)
 
-    def k_copy(n, e, a, b):
-        source = tx if isinstance(e, int) else g.at[e]
+    def k_copy(n, e, a, b, inverse):
+        source = tx if inverse else g.at[e]
         return copy(source, rx.at[8 - n, e], ks.at[n, e], kr.at[8 - n, e], a, b)
 
     def x_copy(h, o):
@@ -145,6 +147,29 @@
             device_id_type=pl.DeviceIdType.MESH,
         )
 
+    def shared(o):
+        oa, ob = unslot(o)
+        found = []
+        for v in range(9):
+            va, vb = unslot(v)
+            if v != o and abs(va - oa) <= 1 and abs(vb - ob) <= 1:
+                found.append((v, (va - oa + 1) * 3 + vb - ob + 1))
+        return found
+
+    empty = jnp.zeros((128, 128), jnp.float32)
+    f[...] = jnp.zeros(f.shape, jnp.float32)
+    g[...] = jnp.zeros(g.shape, jnp.float32)
+    fs[...] = jnp.zeros(fs.shape, jnp.float32)
+    near[...] = jnp.zeros(near.shape, jnp.float32)
+    for o in range(9):
+        if o != 4:
+            rx[o, 4] = empty
+            for _, e in shared(o):
+                rx[o, e] = empty
+    for h in range(5, 9):
+        fx[h - 5, 4] = empty
+        for _, e in shared(h):
+            fx[h - 5, e] = empty
     neighbours(greet)
     line = lax.broadcasted_iota(jnp.int32, (16, 256), 0)
     plain = jnp.where(
@@ -179,7 +204,7 @@
         jnp.int32, (128, 128), 1
     )
 
-    def start_block(source, here, slot):
+    def start_block(source, here):
         where = source[128:136].T
         parts = []
         for s in range(2):
@@ -192,127 +217,122 @@
                     block = block + jnp.where(eye, own[4 + s : 5 + s], 0.0)
                 line.append(block)
             parts.append(jnp.concatenate(line, axis=1))
-        ea[slot] = parts[1] - dot3(split(source[0:128]), split(parts[0]), TN)
-
-    start_block(pack_ref, True, 4)
+        return parts[1] - dot3(split(source[0:128].T), split(parts[0]), NN)
+
+    ea[4] = start_block(pack_ref, True)
     mat[...] = ea[4, :, 128:] - dot3(split(ea[4, :, :128]), own_interp, NN)
-
-    def start(n, a, b):
-        pack_copy(8 - n, -a, -b).wait_recv()
-        start_block(near.at[n], False, n)
-
-    neighbours(start)
+    neighbours(lambda n, a, b: pack_copy(8 - n, -a, -b).wait_recv())
+    for o in range(9):
+        if o != 4:
+            ea[o] = jnp.where(inside(*unslot(o)), start_block(near.at[o], False), 0.0)
 
     def stage(k):
         @pl.when(my_colour == k)
         def _():
             tx[...] = factor128(mat[...])[1]
-            neighbours(lambda n, a, b: k_copy(n, 4, a, b).start())
-
-        def gather_terms(o):
-            oa, ob = unslot(o)
-
-            @pl.when(inside(oa, ob) & (colour(oa, ob) == k))
-            def _():
-                def term(e):
-                    ea_, eb_ = unslot(e)
-                    va, vb = oa + ea_, ob + eb_
-
-                    @pl.when((e != 4) & near_pair(va, vb) & inside(va, vb) & (colour(va, vb) < k))
+            neighbours(lambda n, a, b: k_copy(n, 4, a, b, True).start())
+
+        def process(sources):
+            for o in sources:
+                oa, ob = unslot(o)
+                if o != 4:
+                    for v, e in shared(o):
+                        va, vb = unslot(v)
+
+                        @pl.when(inside(oa, ob) & inside(va, vb) & (colour(va, vb) < k))
+                        def _():
+                            k_copy(8 - o, e, -oa, -ob, False).wait_recv()
+
+            for o in sources:
+                total = ea[o]
+                for v, e in shared(o):
+                    value = g[e] if o == 4 else rx[o, e]
+                    total = total - mm(cat_left(value), cat_right(f[v]))
+                ea[o] = total
+            for o in sources:
+                oa, ob = unslot(o)
+                if o != 4:
+
+                    @pl.when(inside(oa, ob))
                     def _():
-                        right = split(f[(va + 1) * 3 + vb + 1])
-
-                        @pl.when(o == 4)
-                        def _():
-                            ea[o] -= dot3(split(g[e]), right, NN)
-
-                        @pl.when(o != 4)
-                        def _():
-                            k_copy(8 - o, e, -oa, -ob).wait_recv()
-                            ea[o] -= dot3(split(rx[o, e]), right, NN)
-
-                loop(term)
-
-        loop(gather_terms)
-
-        def arrive(o):
-            oa, ob = unslot(o)
-
-            @pl.when(inside(oa, ob) & (colour(oa, ob) == k))
-            def _():
-                @pl.when(o == 4)
-                def _():
-                    acc[...] = dot3(split(tx[...]), split(ea[4]), NN)
-
-                @pl.when(o != 4)
-                def _():
-                    k_copy(8 - o, 4, -oa, -ob).wait_recv()
-                    acc[...] = dot3(split(rx[o, 4]), split(ea[o]), NN)
-
-                f[o] = acc[...]
-                fs[o] = acc[:, :128]
+                        k_copy(8 - o, 4, -oa, -ob, False).wait_recv()
+
+            for o in sources:
+                factor = tx[...] if o == 4 else rx[o, 4]
+                new = mm(cat_left(factor), cat_right(ea[o]))
+                f[o] = new
+                fs[o] = new[:, :128]
+            if sources != [4]:
 
                 @pl.when(my_colour > k)
                 def _():
-                    new = acc[:, 128:] - dot3(split(acc[:, :128]), own_interp, NN)
-                    flip = new.T
-                    g[o] = flip
-                    mat[...] -= dot3(split(flip), split(new), NN)
-
-                    def early(n, a, b):
-                        @pl.when(near_pair(oa - a, ob - b))
+                    total = mat[...]
+                    right = cat_right(pack_ref[0:128])
+                    for o in sources:
+                        new = f[o, :, 128:] - mm(cat_left(f[o, :, :128]), right)
+                        flip = new.T
+                        g[o] = flip
+                        total = total - mm(cat_left(flip), cat_right(new))
+                    mat[...] = total
+                    for o in sources:
+                        oa, ob = unslot(o)
+                        for n in range(9):
+                            a, b = unslot(n)
+                            if n != 4 and abs(oa - a) <= 1 and abs(ob - b) <= 1:
+
+                                @pl.when(inside(a, b) & inside(oa, ob))
+                                def _():
+                                    k_copy(n, o, a, b, False).start()
+
+            for o in sources:
+                oa, ob = unslot(o)
+                for h in range(5, 9):
+                    ha, hb = unslot(h)
+                    if abs(oa + ha) <= 1 and abs(ob + hb) <= 1:
+
+                        @pl.when(inside(-ha, -hb) & inside(oa, ob))
                         def _():
-                            k_copy(n, o, a, b).start()
-
-                    neighbours(early)
-
-                def forward(h):
-                    ha, hb = unslot(h)
-
-                    @pl.when(inside(-ha, -hb) & near_pair(oa + ha, ob + hb))
-                    def _():
-                        x_copy(h, o).start()
-
-                loop(forward, 5, 9)
-
-        loop(arrive)
+                            x_copy(h, o).start()
+
+        for tall_odd in range(2):
+            for wide_odd in range(2):
+                sources = [
+                    (a + 1) * 3 + b + 1
+                    for a in ((-1, 1) if tall_odd else (0,))
+                    for b in ((-1, 1) if wide_odd else (0,))
+                ]
+
+                @pl.when(((row_at + k // 2) % 2 == tall_odd) & ((col_at + k) % 2 == wide_odd))
+                def _():
+                    process(sources)
 
     loop(stage, 0, 4)
 
-    def centre(o):
-        oa, ob = unslot(o)
-
-        @pl.when(inside(oa, ob))
-        def _():
-            part = split(fs[o])
-            acc[:, :128] -= dot3(part, part, TN)
-
-    acc[:, :128] = jnp.where(eye, own[4:5], 0.0)
-    loop(centre)
-    dd[0] = acc[:, :128]
-
-    def pair(h):
+    for h in range(5, 9):
         ha, hb = unslot(h)
-        acc[:, :128] = jnp.zeros((128, 128), jnp.float32)
-
-        @pl.when(inside(ha, hb))
-        def _():
-            def term(o):
-                oa, ob = unslot(o)
-                va, vb = oa - ha, ob - hb
-
-                @pl.when(inside(oa, ob) & near_pair(va, vb))
+        for v in range(9):
+            va, vb = unslot(v)
+            if abs(va - ha) <= 1 and abs(vb - hb) <= 1:
+
+                @pl.when(inside(ha, hb) & inside(va, vb))
                 def _():
-                    e = (va + 1) * 3 + vb + 1
-                    x_copy(h, e).wait_recv()
-                    acc[:, :128] -= dot3(split(fs[o]), split(fx[h - 5, e]), TN)
-
-            loop(term)
-
-        dd[h - 4] = acc[:, :128]
-        dd[h] = acc[:, :128].T
-
-    loop(pair, 5, 9)
+                    x_copy(h, (va - ha + 1) * 3 + vb - hb + 1).wait_recv()
+
+    flips = [cat_left(fs[v].T) for v in range(9)]
+    total = jnp.where(eye, own[4:5], 0.0)
+    for v in range(9):
+        total = total - mm(flips[v], cat_right(fs[v]))
+    dd[0] = total
+    for h in range(5, 9):
+        ha, hb = unslot(h)
+        total = empty
+        for v in range(9):
+            va, vb = unslot(v)
+            if abs(va - ha) <= 1 and abs(vb - hb) <= 1:
+                e = (va - ha + 1) * 3 + vb - hb + 1
+                total = total - mm(flips[v], cat_right(fx[h - 5, e]))
+        dd[h - 4] = total
+        dd[h] = total.T
 
     lane = lax.broadcasted_iota(jnp.int32, (8, 128), 1)
 
@@ -368,7 +388,7 @@
 
             @pl.when(is_sent & near_pair(ea_ - a, eb_ - b))
             def _():
-                k_copy(n, e, a, b).wait_send()
+                k_copy(n, e, a, b, False).wait_send()
 
         loop(each)
 
@@ -482,7 +502,7 @@
     sems,
 ):
     count = SB // 128
-    width = 3 * SB
+    width = 2 * SB
     chunk = 256
     row = lax.broadcasted_iota(jnp.int32, (128, SB), 0)
     col = lax.broadcasted_iota(jnp.int32, (128, SB), 1)
@@ -506,12 +526,12 @@
                 line = turned[16 + l, place - 128 : place - 112]
             table[1, l, n] = shifted_line(line, n)
 
-    def piece(values, wide, which, k, l):
+    def piece(values, wide, which, k, l, token=0.0):
         place = 48 + 8 * which + l
         return root_block(
             wide[k, 0],
             wide[k, 1],
-            turned[16, place : place + 1],
+            turned[16, place : place + 1] + token,
             turned[18, place : place + 1],
             [values[which, l, n, pl.ds(k, 1)] for n in range(9)],
         )
@@ -531,22 +551,23 @@
         return 0
 
     lax.fori_loop(0, count, assemble, 0)
-    for i in range(count):
-        work[128 * i : 128 * i + 128, 2 * SB :] = jnp.where(col == row + 128 * i, 1.0, 0.0)
-    work[SB:] = jnp.zeros((128, width), jnp.float32)
+    work[SB:] = jnp.zeros((128, width + 128), jnp.float32)
+    eye = jnp.where(apart() == 0, 1.0, 0.0)
     diag[...] = work[:128, :128]
     wcur[...] = jnp.zeros((128, 384), jnp.bfloat16)
 
-    def build(k):
-        for l in range(8):
-            cols = slice(128 * l, 128 * l + 128)
-            hi, lo = split(piece(table, rows_ref, 1, k, l))
-            x_hi[rows_of(k), cols] = hi
-            x_lo[rows_of(k), cols] = lo
-            base[rows_of(k), cols] = piece(table, rows_ref, 0, k, l)
+    def build(k, l, token):
+        cols = slice(128 * l, 128 * l + 128)
+        hi, lo = split(piece(table, rows_ref, 1, k, l, token))
+        x_hi[rows_of(k), cols] = hi
+        x_lo[rows_of(k), cols] = lo
+        base[rows_of(k), cols] = piece(table, rows_ref, 0, k, l, token)
 
     def scale(p):
         here = rows_of(p)
+        spot = rows_of(jnp.where(p == count, 2 * count, p))
+        work[:SB, spot] = jnp.zeros((SB, 128), jnp.float32)
+        work[here, spot] = eye
         for c in range(width // chunk):
             cols = slice(c * chunk, c * chunk + chunk)
             new = mm(wcur[...], cat_right(work[here, cols]))
@@ -564,9 +585,7 @@
         for c in range(width // chunk):
             cols = slice(c * chunk, c * chunk + chunk)
             work[:SB, cols] -= mm(left[...], right[:, cols])
-        build(2 * i)
-        build(2 * i + 1)
-        w = factor128(diag[...])[1]
+        w = factor128(diag[...], lambda p, t: build(2 * i + p // 8, p % 8, t))[1]
         wcur[...] = cat_left(w)
         here, after = rows_of(i), rows_of(i + 1)
         u = mm(wcur[...], cat_right(work[here, after]))
@@ -575,7 +594,8 @@
 
     lax.fori_loop(0, count, step, 0)
     last = rows_of(count - 1)
-    for c in range(SB // chunk, width // chunk):
+    work[last, SB - 128 : SB] = eye
+    for c in range(width // chunk):
         cols = slice(c * chunk, c * chunk + chunk)
         work[last, cols] = mm(wcur[...], cat_right(work[last, cols]))
 
@@ -591,7 +611,7 @@
         z_hi[here] = hi
         z_lo[here] = lo
         for j in range(count):
-            hi, lo = split(work[here, 2 * SB + 128 * j : 2 * SB + 128 * j + 128].T)
+            hi, lo = split(jnp.where(j <= i, work[here, 128 * j : 128 * j + 128], 0.0).T)
             there = slice(128 * j, 128 * j + 128)
             wt[0, there, here] = hi
             wt[1, there, here] = lo
@@ -646,11 +666,11 @@
         in_specs=[pl.BlockSpec(memory_space=pltpu.SMEM), vmem, vmem, vmem],
         out_specs=pl.BlockSpec(memory_space=pl.ANY),
         scratch_shapes=[
-            pltpu.VMEM((SB + 128, 3 * SB), jnp.float32),
+            pltpu.VMEM((SB + 128, 2 * SB + 128), jnp.float32),
             pltpu.VMEM((128, 128), jnp.float32),
             pltpu.VMEM((128, 384), jnp.bfloat16),
             pltpu.VMEM((SB, 384), jnp.bfloat16),
-            pltpu.VMEM((384, 3 * SB), jnp.bfloat16),
+            pltpu.VMEM((384, 2 * SB), jnp.bfloat16),
             pltpu.VMEM((2, SB, SB), jnp.bfloat16),
             pltpu.VMEM((SB, SB), jnp.bfloat16),
             pltpu.VMEM((SB, SB), jnp.bfloat16),

time: 226 us -> 213 us (0.942)
  starting transfers between devices: 23.7 us -> 14.9 us
  Pallas kernels: 164 us -> 159 us
    all_to_all x1, starting transfers between devices: 23.7 us -> 14.9 us  [root_phase(): lax.all_to_all(outgoing.reshape(128, 32, 128), ('row', 'col'), split_axis...]
    pallas_call x1, Pallas kernels: 97.4 us -> 93.2 us  [tail_solve(): pl.pallas_call(tail_kernel, out_shape=jax.ShapeDtypeStruct((2048, SB), jn...]
where the time goes in v3:
time: 213 us; the launch traced here: 212 us
  Pallas kernels  159 us (75%)
  waiting for transfers between devices  28.7 us (13%)
  starting transfers between devices  14.9 us (7%)
  local copies, waits for them, and re-layouts  8.46 us (4%)
    pallas_call x1, Pallas kernels, tail_solve(): pl.pallas_call(tail_kernel, out_shape=jax.ShapeDtypeStruct((2048, SB), jn...  93.2 us
    pallas_call x1, Pallas kernels, box_phase(): pl.pallas_call(box_kernel, out_shape=jax.ShapeDtypeStruct((128, 4, 8, 128...  66 us
    all_to_all x1, waiting for transfers between devices, root_phase(): lax.all_to_all(outgoing.reshape(128, 32, 128), ('row', 'col'), split_axis...  28.7 us
    all_to_all x1, starting transfers between devices, root_phase(): lax.all_to_all(outgoing.reshape(128, 32, 128), ('row', 'col'), split_axis...  14.9 us
  transfers between devices with their start and end apart: 1, of which 1 were waited for; matrix products, arithmetic and copies ran while one was open for 0% of the time, Pallas kernels for 0%

profile of v3, /device:TPU:1, one launch (start us, length us, event | category | flops | bytes accessed | tf_op | source)
XLA Modules:
  0.0 212.2 jit_solution(5019977887904951036)
XLA Ops:
  0.0 0.0 copy-start
  0.0 0.8 copy-done
  0.8 0.0 copy-start.1
  0.8 0.7 copy-done.1
  1.5 0.0 copy-start.2
  1.5 0.7 copy-done.2
  2.2 0.0 copy-start.3
  2.2 0.7 copy-done.3
  2.9 66.0 %shard_map.46 = f32[128,4,8,128]{3,2,1,0:T(8,128)} custom-call(f32[2,256]{1,0:T(2,128)S(1)} %bitcast.17, s32[1,256]{1,0:T(1,128)S(1)} %bitcast.18, f32[1,256]{1,0:T(1,128)S(1)} %bitcast.19, f32[128,128]{1,0:T(8,128)S(1)} %bitcast.16), custom_call_target="tpu_custom_call" | custom-call | tf_op jit(solution)/shard_map/pallas_call | solution.py:414
  68.9 14.9 %all-to-all-start = ((f32[128,32,128]{2,1,0:T(8,128)}), f32[128,32,128]{2,1,0:T(8,128)}, u32[]{:S(2)}, u32[]{:S(2)}) async-start(f32[128,32,128]{2,1,0:T(8,128)} %bitcast.6), calls=%async_computation | async-start | bytes 4194304 | tf_op jit(solution)/shard_map/all_to_all | solution.py:689
  83.8 0.7 pad_add_fusion.at_ref
  84.5 28.7 %all-to-all-done = f32[128,32,128]{2,1,0:T(8,128)} async-done(((f32[128,32,128]{2,1,0:T(8,128)}), f32[128,32,128]{2,1,0:T(8,128)}, u32[]{:S(2)}, u32[]{:S(2)}) %all-to-all-start) | async-done | bytes 2097184 | tf_op jit(solution)/shard_map/all_to_all | solution.py:689
  113.2 2.0 copy.8
  115.2 0.0 copy-start.4
  115.3 1.6 broadcast_in_dim.4.lead_ref
  116.9 1.9 broadcast_in_dim.5.rows_ref
  118.8 0.0 copy-done.4
  118.8 93.2 %shard_map.47 = f32[2048,1024]{1,0:T(8,128)} custom-call(s32[2]{0:T(128)} %pad_add_fusion.at_ref, f32[32,128,128]{2,1,0:T(8,128)} %bitcast.22, f32[8,2,128,128]{3,2,1,0:T(8,128)} %broadcast_in_dim.4.lead_ref, f32[16,2,128,128]{3,2,1,0:T(8,128)} %broadcast_in_dim.5.rows_ref), custom_call_target="tpu_custom_call" | custom-call | tf_op jit(solution)/shard_map/pallas_call | solution.py:663
  (6 shorter events, 0.0 us)
Async XLA Ops:
  0.0 0.8 copy-start
  0.8 0.7 copy-start.1
  1.5 0.7 copy-start.2
  2.2 0.7 copy-start.3
  68.9 44.3 %all-to-all-start = ((f32[128,32,128]{2,1,0:T(8,128)}), f32[128,32,128]{2,1,0:T(8,128)}, u32[]{:S(2)}, u32[]{:S(2)}) async-start(f32[128,32,128]{2,1,0:T(8,128)} %bitcast.6), calls=%async_computation | async-start | bytes 4194304 | tf_op jit(solution)/shard_map/all_to_all | solution.py:689
  115.2 3.6 %copy-start.4 = (f32[128,32,128]{0,2,1:T(8,128)}, f32[128,32,128]{0,2,1:T(8,128)S(1)}, u32[]{:S(2)}) copy-start(f32[128,32,128]{0,2,1:T(8,128)S(1)} %copy.8) | copy-start | bytes 6291460

commit v4 on v3

--- a/solution.py
+++ b/solution.py
@@ -80,7 +80,7 @@
 NT = ((1,), (1,))
 
 
-def box_kernel(off_ref, order_ref, nug_ref, interp_ref, out_ref, pack_ref, near, ea, f, fs, g, mat, acc, tx, rx, fx, dd, ps, pr, ks, kr, xs, xr):
+def box_kernel(off_ref, order_ref, nug_ref, interp_ref, out_ref, pack_ref, upper, near, ea, f, fs, g, mat, acc, tx, rx, fx, dd, ps, pr, ks, kr, xs, xr):
     row_at = lax.axis_index("row")
     col_at = lax.axis_index("col")
     row_count = lax.axis_size("row")
@@ -126,8 +126,15 @@
 
         loop(each)
 
-    def pack_copy(n, a, b):
-        return copy(pack_ref, near.at[8 - n], ps.at[n], pr.at[8 - n], a, b)
+    def place_copy(n, a, b):
+        part = pl.ds(128, 8)
+        return copy(
+            pack_ref.at[part], near.at[8 - n, part], ps.at[0, n], pr.at[0, 8 - n], a, b
+        )
+
+    def interp_copy(n, a, b):
+        part = pl.ds(0, 128)
+        return copy(interp_ref, near.at[8 - n, part], ps.at[1, n], pr.at[1, 8 - n], a, b)
 
     def k_copy(n, e, a, b, inverse):
         source = tx if inverse else g.at[e]
@@ -196,7 +203,8 @@
     tall = 1 + lax.min(row_at, 1) + lax.min(row_count - 1 - row_at, 1)
     wide = 1 + lax.min(col_at, 1) + lax.min(col_count - 1 - col_at, 1)
     pl.semaphore_wait(barrier, tall * wide - 1)
-    neighbours(lambda n, a, b: pack_copy(n, a, b).start())
+    neighbours(lambda n, a, b: place_copy(n, a, b).start())
+    neighbours(lambda n, a, b: interp_copy(n, a, b).start())
 
     own_interp = split(pack_ref[0:128])
     my_colour = colour(0, 0)
@@ -217,17 +225,31 @@
                     block = block + jnp.where(eye, own[4 + s : 5 + s], 0.0)
                 line.append(block)
             parts.append(jnp.concatenate(line, axis=1))
-        return parts[1] - dot3(split(source[0:128].T), split(parts[0]), NN)
-
-    ea[4] = start_block(pack_ref, True)
+        return parts
+
+    def reduce_rows(upper, lower, source):
+        return lower - mm(cat_left(source[0:128].T), cat_right(upper))
+
+    ea[4] = reduce_rows(*start_block(pack_ref, True), pack_ref)
     mat[...] = ea[4, :, 128:] - dot3(split(ea[4, :, :128]), own_interp, NN)
-    neighbours(lambda n, a, b: pack_copy(8 - n, -a, -b).wait_recv())
+
+    @pl.when(my_colour == 0)
+    def _():
+        tx[...] = factor128(mat[...])[1]
+        neighbours(lambda n, a, b: k_copy(n, 4, a, b, True).start())
+
+    neighbours(lambda n, a, b: place_copy(8 - n, -a, -b).wait_recv())
     for o in range(9):
         if o != 4:
-            ea[o] = jnp.where(inside(*unslot(o)), start_block(near.at[o], False), 0.0)
+            upper[o], ea[o] = start_block(near.at[o], False)
+    neighbours(lambda n, a, b: interp_copy(8 - n, -a, -b).wait_recv())
+    for o in range(9):
+        if o != 4:
+            value = reduce_rows(upper[o], ea[o], near.at[o])
+            ea[o] = jnp.where(inside(*unslot(o)), value, 0.0)
 
     def stage(k):
-        @pl.when(my_colour == k)
+        @pl.when((my_colour == k) & (k > 0))
         def _():
             tx[...] = factor128(mat[...])[1]
             neighbours(lambda n, a, b: k_copy(n, 4, a, b, True).start())
@@ -380,7 +402,8 @@
             out_ref[dest, 3] = tail
 
     def finish(n, a, b):
-        pack_copy(n, a, b).wait_send()
+        place_copy(n, a, b).wait_send()
+        interp_copy(n, a, b).wait_send()
 
         def each(e):
             ea_, eb_ = unslot(e)
@@ -418,6 +441,7 @@
         out_specs=pl.BlockSpec(memory_space=pltpu.VMEM),
         scratch_shapes=[
             pltpu.VMEM((136, 128), jnp.float32),
+            pltpu.VMEM((9, 128, 256), jnp.float32),
             pltpu.VMEM((9, 136, 128), jnp.float32),
             pltpu.VMEM((9, 128, 256), jnp.float32),
             pltpu.VMEM((9, 128, 256), jnp.float32),
@@ -429,8 +453,8 @@
             pltpu.VMEM((9, 9) + block, jnp.float32),
             pltpu.VMEM((4, 9) + block, jnp.float32),
             pltpu.VMEM((9,) + block, jnp.float32),
-            pltpu.SemaphoreType.DMA((9,)),
-            pltpu.SemaphoreType.DMA((9,)),
+            pltpu.SemaphoreType.DMA((2, 9)),
+            pltpu.SemaphoreType.DMA((2, 9)),
             pltpu.SemaphoreType.DMA((9, 9)),
             pltpu.SemaphoreType.DMA((9, 9)),
             pltpu.SemaphoreType.DMA((4, 9)),
@@ -483,9 +507,9 @@
 def tail_kernel(
     at_ref,
     turned,
+    out_ref,
     lead_ref,
     rows_ref,
-    out_ref,
     work,
     diag,
     wcur,
@@ -536,6 +560,15 @@
             [values[which, l, n, pl.ds(k, 1)] for n in range(9)],
         )
 
+    xs = turned[16, 32:64].T
+    ys = turned[18, 32:64].T
+    for k in range(16):
+        rows_ref[k, 0] = jnp.broadcast_to(xs[:, k : k + 1], (128, 128))
+        rows_ref[k, 1] = jnp.broadcast_to(ys[:, k : k + 1], (128, 128))
+    for k in range(8):
+        lead_ref[k, 0] = jnp.broadcast_to(xs[:, 24 + k : 25 + k], (128, 128))
+        lead_ref[k, 1] = jnp.broadcast_to(ys[:, 24 + k : 25 + k], (128, 128))
+
     def assemble(k, _):
         for l in range(8):
             work[rows_of(k), SB + 128 * l : SB + 128 * l + 128] = piece(tab, lead_ref, 0, k, l)
@@ -576,8 +609,16 @@
             for j in range(chunk // 128):
                 n = c * (chunk // 128) + j
                 if n < count:
-                    part = jnp.where(p < n, new[:, 128 * j : 128 * j + 128], 0.0)
-                    left[128 * n : 128 * n + 128] = cat_left(part.T)
+                    flip = new[:, 128 * j : 128 * j + 128].T
+                    there = slice(128 * n, 128 * n + 128)
+                    left[there] = cat_left(jnp.where(p < n, flip, 0.0))
+                    hi, lo = split(jnp.where(p < n, 0.0, flip))
+                    wt[0, there, here] = hi
+                    wt[1, there, here] = lo
+            if c * chunk >= SB:
+                hi, lo = split(new)
+                z_hi[here, c * chunk - SB : c * chunk - SB + chunk] = hi
+                z_lo[here, c * chunk - SB : c * chunk - SB + chunk] = lo
 
     def step(i, _):
         p = jnp.where(i == 0, count, i - 1)
@@ -593,34 +634,18 @@
         return 0
 
     lax.fori_loop(0, count, step, 0)
-    last = rows_of(count - 1)
-    work[last, SB - 128 : SB] = eye
-    for c in range(width // chunk):
-        cols = slice(c * chunk, c * chunk + chunk)
-        work[last, cols] = mm(wcur[...], cat_right(work[last, cols]))
-
-    def flip(i, _):
-        here = rows_of(i)
-
-        @pl.when(at_ref[1] == 0)
-        def _():
-            work[here, SB : 2 * SB] = jnp.where(col == row + 128 * i, -1.0, 0.0)
-
-        hi, lo = split(work[here, SB : 2 * SB])
-        right[0:128, :SB] = hi
-        z_hi[here] = hi
-        z_lo[here] = lo
-        for j in range(count):
-            hi, lo = split(jnp.where(j <= i, work[here, 128 * j : 128 * j + 128], 0.0).T)
-            there = slice(128 * j, 128 * j + 128)
-            wt[0, there, here] = hi
-            wt[1, there, here] = lo
-        return 0
-
-    lax.fori_loop(0, count, flip, 0)
+    scale(count - 1)
+
+    @pl.when(at_ref[1] == 0)
+    def _():
+        for i in range(count):
+            here = slice(128 * i, 128 * i + 128)
+            z_hi[here] = jnp.where(col == row + 128 * i, -1.0, 0.0).astype(jnp.bfloat16)
+            z_lo[here] = jnp.zeros((128, SB), jnp.bfloat16)
+
     for c in range(SB // chunk):
         cols = slice(c * chunk, c * chunk + chunk)
-        y_hi, y_lo = z_hi[:, cols], z_lo[:, cols]
+        y_hi, y_lo = z_hi[:SB, cols], z_lo[:SB, cols]
         for m in range(4):
             some = slice(m * 256, m * 256 + 256)
             deep = slice(m * 256, SB)
@@ -641,9 +666,9 @@
         for c in range(SB // chunk):
             cols = slice(c * chunk, c * chunk + chunk)
             part = (
-                mm(x_hi[here], z_lo[:, cols])
-                + mm(x_lo[here], z_hi[:, cols])
-                + mm(x_hi[here], z_hi[:, cols])
+                mm(x_hi[here], z_lo[:SB, cols])
+                + mm(x_lo[here], z_hi[:SB, cols])
+                + mm(x_hi[here], z_hi[:SB, cols])
             )
             value = jnp.where(at_ref[1] == 0, 0.0, base[here, cols]) - part
             down = (at_ref[0] * 4 + r) * tall + lax.broadcasted_iota(jnp.int32, value.shape, 0)
@@ -658,22 +683,24 @@
         pltpu.make_async_copy(base.at[here], out_ref.at[here], sems.at[r]).wait()
 
 
-def tail_solve(at, turned, lead, rows_wide):
+def tail_solve(at, turned):
     vmem = pl.BlockSpec(memory_space=pltpu.VMEM)
     return pl.pallas_call(
         tail_kernel,
         out_shape=jax.ShapeDtypeStruct((2048, SB), jnp.float32),
-        in_specs=[pl.BlockSpec(memory_space=pltpu.SMEM), vmem, vmem, vmem],
+        in_specs=[pl.BlockSpec(memory_space=pltpu.SMEM), vmem],
         out_specs=pl.BlockSpec(memory_space=pl.ANY),
         scratch_shapes=[
+            pltpu.VMEM((8, 2, 128, 128), jnp.float32),
+            pltpu.VMEM((16, 2, 128, 128), jnp.float32),
             pltpu.VMEM((SB + 128, 2 * SB + 128), jnp.float32),
             pltpu.VMEM((128, 128), jnp.float32),
             pltpu.VMEM((128, 384), jnp.bfloat16),
             pltpu.VMEM((SB, 384), jnp.bfloat16),
             pltpu.VMEM((384, 2 * SB), jnp.bfloat16),
-            pltpu.VMEM((2, SB, SB), jnp.bfloat16),
-            pltpu.VMEM((SB, SB), jnp.bfloat16),
-            pltpu.VMEM((SB, SB), jnp.bfloat16),
+            pltpu.VMEM((2, SB, SB + 128), jnp.bfloat16),
+            pltpu.VMEM((SB + 128, SB), jnp.bfloat16),
+            pltpu.VMEM((SB + 128, SB), jnp.bfloat16),
             pltpu.VMEM((2048, SB), jnp.bfloat16),
             pltpu.VMEM((2048, SB), jnp.bfloat16),
             pltpu.VMEM((2048, SB), jnp.float32),
@@ -682,7 +709,7 @@
             pltpu.SemaphoreType.DMA((4,)),
         ],
         compiler_params=pltpu.CompilerParams(vmem_limit_bytes=60 * 2**20),
-    )(at, turned, lead, rows_wide)
+    )(at, turned)
 
 
 def root_phase(outgoing, row_at, col_at):
@@ -691,11 +718,7 @@
     )
     turned = jnp.transpose(arrived, (1, 2, 0))
 
-    def wide(start, size):
-        part = jnp.stack([turned[16, start : start + size], turned[18, start : start + size]], axis=1)
-        return jnp.broadcast_to(part[:, :, :, None], part.shape + (128,))
-
-    return tail_solve(jnp.stack([row_at, col_at]), turned, wide(56, 8), wide(32, 16))
+    return tail_solve(jnp.stack([row_at, col_at]), turned)
 
 
 def on_device(offsets, point_order, nugget, interp):

time: 213 us -> 199 us (0.934)
  Pallas kernels: 159 us -> 151 us
  local copies, waits for them, and re-layouts: 8.46 us -> 4.79 us
    pallas_call x1, Pallas kernels: 66 us -> 60.4 us  [box_phase(): pl.pallas_call(box_kernel, out_shape=jax.ShapeDtypeStruct((128, 4, 8, 128...]
    broadcast_in_dim x2 -> x0, local copies, waits for them, and re-layouts: 3.55 us -> none  [wide(): return jnp.broadcast_to(part[:, :, :, None], part.shape + (128,))]
    pallas_call x1, Pallas kernels: 93.2 us -> 90.8 us  [tail_solve(): pl.pallas_call(tail_kernel, out_shape=jax.ShapeDtypeStruct((2048, SB), jn...]
where the time goes in v4:
time: 199 us
  Pallas kernels  151 us (76%)
  waiting for transfers between devices  29.1 us (15%)
  starting transfers between devices  13 us (7%)
  local copies, waits for them, and re-layouts  4.79 us (2%)
    pallas_call x1, Pallas kernels, tail_solve(): pl.pallas_call(tail_kernel, out_shape=jax.ShapeDtypeStruct((2048, SB), jn...  90.8 us
    pallas_call x1, Pallas kernels, box_phase(): pl.pallas_call(box_kernel, out_shape=jax.ShapeDtypeStruct((128, 4, 8, 128...  60.4 us
    all_to_all x1, waiting for transfers between devices, root_phase(): lax.all_to_all(outgoing.reshape(128, 32, 128), ('row', 'col'), split_axis...  29.1 us
    all_to_all x1, starting transfers between devices, root_phase(): lax.all_to_all(outgoing.reshape(128, 32, 128), ('row', 'col'), split_axis...  13 us
  transfers between devices with their start and end apart: 1, of which 1 were waited for; matrix products, arithmetic and copies ran while one was open for 0% of the time, Pallas kernels for 0%

profile of v4, /device:TPU:1, one launch (start us, length us, event | category | flops | bytes accessed | tf_op | source)
XLA Modules:
  0.0 199.0 jit_solution(6945252738399593255)
XLA Ops:
  0.0 0.0 copy-start
  0.0 0.8 copy-done
  0.8 0.0 copy-start.1
  0.8 0.7 copy-done.1
  1.5 0.0 copy-start.2
  1.5 0.7 copy-done.2
  2.2 0.0 copy-start.3
  2.2 0.7 copy-done.3
  2.9 60.4 %shard_map.46 = f32[128,4,8,128]{3,2,1,0:T(8,128)} custom-call(f32[2,256]{1,0:T(2,128)S(1)} %bitcast.9, s32[1,256]{1,0:T(1,128)S(1)} %bitcast.10, f32[1,256]{1,0:T(1,128)S(1)} %bitcast.11, f32[128,128]{1,0:T(8,128)S(1)} %bitcast.8), custom_call_target="tpu_custom_call" | custom-call | tf_op jit(solution)/shard_map/pallas_call | solution.py:437
  63.3 13.0 %all-to-all-start = ((f32[128,32,128]{2,1,0:T(8,128)}), f32[128,32,128]{2,1,0:T(8,128)S(1)}, u32[]{:S(2)}, u32[]{:S(2)}) async-start(f32[128,32,128]{2,1,0:T(8,128)} %bitcast.6), calls=%async_computation | async-start | bytes 4194304 | tf_op jit(solution)/shard_map/all_to_all | solution.py:716
  76.3 0.6 pad_add_fusion.at_ref
  76.9 29.1 %all-to-all-done = f32[128,32,128]{2,1,0:T(8,128)S(1)} async-done(((f32[128,32,128]{2,1,0:T(8,128)}), f32[128,32,128]{2,1,0:T(8,128)S(1)}, u32[]{:S(2)}, u32[]{:S(2)}) %all-to-all-start) | async-done | bytes 2097184 | tf_op jit(solution)/shard_map/all_to_all | solution.py:716
  106.1 1.9 copy.6
  108.0 90.8 %shard_map.47 = f32[2048,1024]{1,0:T(8,128)} custom-call(s32[2]{0:T(128)} %pad_add_fusion.at_ref, f32[32,128,128]{2,1,0:T(8,128)} %bitcast.12), custom_call_target="tpu_custom_call" | custom-call | tf_op jit(solution)/shard_map/pallas_call | solution.py:688
Async XLA Ops:
  0.0 0.8 copy-start
  0.8 0.7 copy-start.1
  1.5 0.7 copy-start.2
  2.2 0.7 copy-start.3
  63.3 42.8 %all-to-all-start = ((f32[128,32,128]{2,1,0:T(8,128)}), f32[128,32,128]{2,1,0:T(8,128)S(1)}, u32[]{:S(2)}, u32[]{:S(2)}) async-start(f32[128,32,128]{2,1,0:T(8,128)} %bitcast.6), calls=%async_computation | async-start | bytes 4194304 | tf_op jit(solution)/shard_map/all_to_all | solution.py:716

commit v5 on v4

--- a/solution.py
+++ b/solution.py
@@ -26,10 +26,12 @@
     for p in range(G):
         q, qw = rows[p], w[p]
         cols = [lcol(q, 8*p+t) for t in range(8)]
+        first = jnp.where(sub == 8, q, srow(q, 0))
+        tops = [lcol(first, 8*p+t) for t in range(8)]
         u, uw, dv = q, qw, None
         for t in range(8):
             pr, pw = srow(q, t), srow(qw, t)
-            d = srow(cols[t], t)
+            d = tops[0] if t == 0 else srow(cols[t], t)
             here = sub == t
             u = pr if t == 0 else jnp.where(here, pr, u)
             uw = pw if t == 0 else jnp.where(here, pw, uw)
@@ -38,7 +40,7 @@
             q = q - m * pr
             qw = qw - m * pw
             for v in range(t + 1, 8):
-                cols[v] = cols[v] - m * srow(cols[v], t)
+                cols[v] = cols[v] - m * (tops[v] if t == 0 else srow(cols[v], t))
         if side is not None:
             side(p, jnp.minimum(jnp.abs(dv[0:1]), 0.0))
         r = lax.rsqrt(dv)
@@ -80,7 +82,8 @@
 NT = ((1,), (1,))
 
 
-def box_kernel(off_ref, order_ref, nug_ref, interp_ref, out_ref, pack_ref, upper, near, ea, f, fs, g, mat, acc, tx, rx, fx, dd, ps, pr, ks, kr, xs, xr):
+def box_kernel(
+    off_in, order_in, nug_in, interp_in, out_ref, off_ref, order_ref, nug_ref, interp_ref, arrive_sem, pack_ref, upper, near, ea, f, fs, g, mat, acc, tx, rx, fx, dd, ps, pr, ks, kr, xs, xr):
     row_at = lax.axis_index("row")
     col_at = lax.axis_index("col")
     row_count = lax.axis_size("row")
@@ -163,6 +166,19 @@
                 found.append((v, (va - oa + 1) * 3 + vb - ob + 1))
         return found
 
+    loads = [
+        pltpu.make_async_copy(source, target, arrive_sem.at[n])
+        for n, (source, target) in enumerate(
+            [
+                (off_in, off_ref),
+                (order_in, order_ref),
+                (nug_in, nug_ref),
+                (interp_in, interp_ref),
+            ]
+        )
+    ]
+    for load in loads:
+        load.start()
     empty = jnp.zeros((128, 128), jnp.float32)
     f[...] = jnp.zeros(f.shape, jnp.float32)
     g[...] = jnp.zeros(g.shape, jnp.float32)
@@ -178,6 +194,8 @@
         for _, e in shared(h):
             fx[h - 5, e] = empty
     neighbours(greet)
+    for load in loads:
+        load.wait()
     line = lax.broadcasted_iota(jnp.int32, (16, 256), 0)
     plain = jnp.where(
         line == 0,
@@ -437,9 +455,14 @@
     return pl.pallas_call(
         box_kernel,
         out_shape=jax.ShapeDtypeStruct((128, 4, 8, 128), jnp.float32),
-        in_specs=[pl.BlockSpec(memory_space=pltpu.VMEM)] * 4,
+        in_specs=[pl.BlockSpec(memory_space=pltpu.HBM)] * 4,
         out_specs=pl.BlockSpec(memory_space=pltpu.VMEM),
         scratch_shapes=[
+            pltpu.VMEM((2, 256), jnp.float32),
+            pltpu.VMEM((1, 256), jnp.int32),
+            pltpu.VMEM((1, 256), jnp.float32),
+            pltpu.VMEM(block, jnp.float32),
+            pltpu.SemaphoreType.DMA((4,)),
             pltpu.VMEM((136, 128), jnp.float32),
             pltpu.VMEM((9, 128, 256), jnp.float32),
             pltpu.VMEM((9, 136, 128), jnp.float32),
@@ -461,7 +484,7 @@
             pltpu.SemaphoreType.DMA((4, 9)),
         ],
         compiler_params=pltpu.CompilerParams(
-            collective_id=0, has_side_effects=True, vmem_limit_bytes=40 * 2**20
+            collective_id=0, has_side_effects=True, vmem_limit_bytes=67043328
         ),
     )(off, order, nug, interp)
 

time: 199 us -> 190 us (0.955)
  Pallas kernels: 151 us -> 145 us
  local copies, waits for them, and re-layouts: 4.79 us -> 1.92 us
    pallas_call x1, Pallas kernels: 90.8 us -> 84.8 us  [tail_solve(): pl.pallas_call(tail_kernel, out_shape=jax.ShapeDtypeStruct((2048, SB), jn...]
    unnamed x8 -> x0, local copies, waits for them, and re-layouts: 2.88 us -> none
where the time goes in v5:
time: 190 us
  Pallas kernels  145 us (76%)
  waiting for transfers between devices  29.1 us (15%)
  starting transfers between devices  13 us (7%)
  local copies, waits for them, and re-layouts  1.92 us (1%)
    pallas_call x1, Pallas kernels, tail_solve(): pl.pallas_call(tail_kernel, out_shape=jax.ShapeDtypeStruct((2048, SB), jn...  84.8 us
    pallas_call x1, Pallas kernels, box_phase(): pl.pallas_call(box_kernel, out_shape=jax.ShapeDtypeStruct((128, 4, 8, 128...  60.1 us
    all_to_all x1, waiting for transfers between devices, root_phase(): lax.all_to_all(outgoing.reshape(128, 32, 128), ('row', 'col'), split_axis...  29.1 us
    all_to_all x1, starting transfers between devices, root_phase(): lax.all_to_all(outgoing.reshape(128, 32, 128), ('row', 'col'), split_axis...  13 us
  transfers between devices with their start and end apart: 1, of which 1 were waited for; matrix products, arithmetic and copies ran while one was open for 0% of the time, Pallas kernels for 0%

profile of v5, /device:TPU:1, one launch (start us, length us, event | category | flops | bytes accessed | tf_op | source)
XLA Modules:
  0.0 189.8 jit_solution(11522242778641067826)
XLA Ops:
  0.0 60.1 %shard_map.46 = f32[128,4,8,128]{3,2,1,0:T(8,128)} custom-call(f32[2,256]{1,0:T(2,128)} %bitcast.11, s32[1,256]{1,0:T(1,128)} %bitcast.12, f32[1,256]{1,0:T(1,128)} %bitcast.13, f32[128,128]{1,0:T(8,128)} %bitcast.10), custom_call_target="tpu_custom_call" | custom-call | tf_op jit(solution)/shard_map/pallas_call | solution.py:455
  60.1 13.0 %all-to-all-start = ((f32[128,32,128]{2,1,0:T(8,128)}), f32[128,32,128]{2,1,0:T(8,128)S(1)}, u32[]{:S(2)}, u32[]{:S(2)}) async-start(f32[128,32,128]{2,1,0:T(8,128)} %bitcast.8), calls=%async_computation | async-start | bytes 4194304 | tf_op jit(solution)/shard_map/all_to_all | solution.py:739
  73.1 0.6 pad_add_fusion.at_ref
  73.7 29.1 %all-to-all-done = f32[128,32,128]{2,1,0:T(8,128)S(1)} async-done(((f32[128,32,128]{2,1,0:T(8,128)}), f32[128,32,128]{2,1,0:T(8,128)S(1)}, u32[]{:S(2)}, u32[]{:S(2)}) %all-to-all-start) | async-done | bytes 2097184 | tf_op jit(solution)/shard_map/all_to_all | solution.py:739
  102.8 1.9 %copy.6 = f32[128,32,128]{0,2,1:T(8,128)} copy(f32[128,32,128]{2,1,0:T(8,128)S(1)} %all-to-all-done) | data formatting | bytes 4194304 | tf_op jit(solution)/shard_map/all_to_all | solution.py:739
  104.7 84.8 %shard_map.47 = f32[2048,1024]{1,0:T(8,128)} custom-call(s32[2]{0:T(128)} %pad_add_fusion.at_ref, f32[32,128,128]{2,1,0:T(8,128)} %bitcast.9), custom_call_target="tpu_custom_call" | custom-call | tf_op jit(solution)/shard_map/pallas_call | solution.py:711
Async XLA Ops:
  60.1 42.7 %all-to-all-start = ((f32[128,32,128]{2,1,0:T(8,128)}), f32[128,32,128]{2,1,0:T(8,128)S(1)}, u32[]{:S(2)}, u32[]{:S(2)}) async-start(f32[128,32,128]{2,1,0:T(8,128)} %bitcast.8), calls=%async_computation | async-start | bytes 4194304 | tf_op jit(solution)/shard_map/all_to_all | solution.py:739
